TPU v7x, 32 devices: a whole 2x2x4 slice. The times are simulated.
32 devices in a mesh: seq: 32 (over z, y, x, core).
Axes of the slice: x: 2, y: 2, z: 4, core: 2. Of those that a mesh axis runs over, the one named last changes fastest.
Arguments:
- queries: bfloat16 [5120, 1024], P('seq'), may hold values from -8 to 8
- key_rows: bfloat16 [5120, 1024], P('seq'), may hold values from -8 to 8
- value_rows: bfloat16 [5120, 1024], P('seq'), may hold values from -6 to 6
- out_weight: bfloat16 [1048576], P('seq'), may hold values from -0.75 to 0.75
- cotangent: bfloat16 [5120, 1024], P('seq'), may hold values from -6 to 6
- row_lengths: int32 [25], replicated, may hold values from 1 to 400, 5120 in all
- window_shift: int32 [5120], P('seq'), may hold values from 0 to 720
Outputs:
- layer_out: bfloat16 [5120, 1024], P('seq')
- grad_queries: bfloat16 [5120, 1024], P('seq')
- grad_keys: bfloat16 [5120, 1024], P('seq')
- grad_values: bfloat16 [5120, 1024], P('seq')
- grad_weight: float32 [1048576], P('seq')
All inputs are finite; a program needn't handle non-finite values.
Results may differ from a plain program's by a relative error of at most 0.025.
Values may be sent and summed in bfloat16 or wider, within the bound.
No kernel may reach another device: no remote copies, remote signals or barrier semaphores. Data moves between devices by JAX's collectives and lax.ppermute only.
A program may use at most 128 MiB of HBM per device.

v0:
```python
import math

import jax
import jax.numpy as jnp
from jax import lax
from jax.sharding import PartitionSpec as P

D = 1024
HEADS = 16
HEAD = 64
WIN = 1120


def as_sent(shard):

    def short(part):
        return part.astype(jnp.bfloat16) if part.dtype == jnp.float32 else part

    return jax.tree.map(short, shard)


def passed_along(block, axis, distance):
    devices = range(lax.axis_size(axis))
    route = [(i - distance, i) for i in devices if i - distance in devices]
    return lax.ppermute(block, axis, route)


def head_view(block):
    return block.reshape(block.shape[0], -1, HEAD)


def window_starts(row_lengths, window_shift, first_point, all_points):
    point_index = first_point + jnp.arange(window_shift.shape[0], dtype=jnp.int32)
    row_ends = jnp.cumsum(row_lengths)
    passed = row_ends[None, :] <= point_index[:, None]
    row_first = jnp.sum(jnp.where(passed, row_lengths[None, :], 0), axis=1)
    return jnp.clip(row_first - window_shift, 0, all_points - WIN)


def join_rows(pieces):
    return jax.tree.map(lambda *blocks: jnp.concatenate(blocks, 0), *pieces)


def cut_rows(tree, begin, end):
    return jax.tree.map(lambda block: block[begin:end], tree)


def stacked_rims(payload, shifter, rim_reach, point_rows):
    extent = rim_reach * point_rows
    lower_rims = payload
    upper_rims = payload
    for level in range(rim_reach.bit_length()):
        covered = 1 << level
        lower_rims = join_rows([shifter(lower_rims, covered), lower_rims])
        upper_rims = join_rows([upper_rims, shifter(upper_rims, -covered)])
    stacked = jax.tree.leaves(lower_rims)[0].shape[0]
    lower_rims = cut_rows(lower_rims, stacked - point_rows - extent, stacked - point_rows)
    upper_rims = cut_rows(upper_rims, point_rows, point_rows + extent)
    return join_rows([lower_rims, payload, upper_rims])


def move_keys(payload, distance):
    return jax.tree.map(
        lambda part, own: part.astype(own.dtype),
        passed_along(as_sent(payload), "seq", distance),
        payload,
    )


def move_queries(payload, distance):
    return jax.tree.map(
        lambda part, own: part.astype(own.dtype),
        passed_along(as_sent(payload), "seq", distance),
        payload,
    )


def move_stats(payload, distance):
    return passed_along(payload, "seq", distance)


def column_slice(block, group_index, group_cols):
    return head_view(lax.dynamic_slice_in_dim(block, group_index * group_cols, group_cols, 1))


def head_pair(table, group_index):
    return lax.dynamic_slice_in_dim(table, group_index * 2, 2, 1).T[:, :, None]


def per_device(queries, key_rows, value_rows, out_weight, cotangent, row_lengths, window_shift):
    point_rows = queries.shape[0]
    devices = lax.axis_size("seq")
    all_points = point_rows * devices
    rim_reach = (WIN - 2 + point_rows) // point_rows
    rim_rows = (2 * rim_reach + 1) * point_rows
    head_scale = 1.0 / math.sqrt(HEAD)
    group_cols = 2 * HEAD
    groups = HEADS // 2
    group_list = jnp.arange(groups, dtype=jnp.int32)
    first_point = lax.axis_index("seq") * point_rows
    starts = window_starts(row_lengths, window_shift, first_point, all_points)
    rim_index = first_point - rim_reach * point_rows + jnp.arange(rim_rows, dtype=jnp.int32)
    own_index = first_point + jnp.arange(point_rows, dtype=jnp.int32)
    allowed = (rim_index[None, :] >= starts[:, None]) & (rim_index[None, :] < starts[:, None] + WIN)
    gathered = lax.all_gather(out_weight, "seq", axis=0, tiled=True).reshape(D, D)
    key_rims, value_rims = stacked_rims((key_rows, value_rows), move_keys, rim_reach, point_rows)

    def forward_group(group_index):
        query_part = column_slice(queries, group_index, group_cols)
        key_part = column_slice(key_rims, group_index, group_cols)
        value_part = column_slice(value_rims, group_index, group_cols)
        scores = (
            jnp.einsum("qhd,khd->hqk", query_part, key_part, preferred_element_type=jnp.float32)
            * head_scale
        )
        scores = jnp.where(allowed[None], scores, -jnp.inf)
        row_top = jnp.max(scores, axis=2, keepdims=True)
        log_total = row_top + jnp.log(jnp.sum(jnp.exp(scores - row_top), axis=2, keepdims=True))
        softmax_out = jnp.exp(scores - log_total).astype(jnp.bfloat16)
        mixed = jnp.einsum(
            "hqk,khd->qhd", softmax_out, value_part, preferred_element_type=jnp.float32
        )
        return (mixed.reshape(point_rows, group_cols).astype(jnp.bfloat16), log_total[:, :, 0])

    mixed_groups, total_groups = lax.map(forward_group, group_list)
    mixed = jnp.transpose(mixed_groups, (1, 0, 2)).reshape(point_rows, D)
    log_total = total_groups.reshape(HEADS, point_rows).T
    layer_out = jnp.dot(mixed, gathered, preferred_element_type=jnp.float32).astype(jnp.bfloat16)
    grad_mixed = lax.dot_general(
        cotangent, gathered, (((1,), (1,)), ((), ())), preferred_element_type=jnp.float32
    ).astype(jnp.bfloat16)
    row_delta = jnp.sum(
        (grad_mixed.astype(jnp.float32) * mixed.astype(jnp.float32)).reshape(
            point_rows, HEADS, HEAD
        ),
        axis=2,
    )
    weight_term = lax.dot_general(
        mixed, cotangent, (((0,), (0,)), ((), ())), preferred_element_type=jnp.float32
    ) * (1.0 / math.sqrt(all_points))
    grad_weight = lax.psum_scatter(
        weight_term.reshape(D * D), "seq", scatter_dimension=0, tiled=True
    )

    def query_group(group_index):
        query_part = column_slice(queries, group_index, group_cols)
        key_part = column_slice(key_rims, group_index, group_cols)
        value_part = column_slice(value_rims, group_index, group_cols)
        grad_part = column_slice(grad_mixed, group_index, group_cols)
        scores = (
            jnp.einsum("qhd,khd->hqk", query_part, key_part, preferred_element_type=jnp.float32)
            * head_scale
        )
        scores = jnp.where(allowed[None], scores, -jnp.inf)
        chances = jnp.exp(scores - head_pair(log_total, group_index))
        grad_scores = jnp.einsum(
            "qhd,khd->hqk", grad_part, value_part, preferred_element_type=jnp.float32
        )
        slopes = (chances * (grad_scores - head_pair(row_delta, group_index))).astype(jnp.bfloat16)
        grad_query = (
            jnp.einsum("hqk,khd->qhd", slopes, key_part, preferred_element_type=jnp.float32)
            * head_scale
        )
        return grad_query.reshape(point_rows, group_cols).astype(jnp.bfloat16)

    grad_queries = jnp.transpose(lax.map(query_group, group_list), (1, 0, 2)).reshape(point_rows, D)
    query_rims, grad_rims = stacked_rims((queries, grad_mixed), move_queries, rim_reach, point_rows)
    total_rims, delta_rims, start_rims = stacked_rims(
        (log_total, row_delta, starts.astype(jnp.float32)), move_stats, rim_reach, point_rows
    )
    rim_starts = start_rims.astype(jnp.int32)
    in_range = (rim_index >= 0) & (rim_index < all_points)
    allowed_back = (
        in_range[:, None]
        & (own_index[None, :] >= rim_starts[:, None])
        & (own_index[None, :] < rim_starts[:, None] + WIN)
    )

    def key_group(group_index):
        query_part = column_slice(query_rims, group_index, group_cols)
        grad_part = column_slice(grad_rims, group_index, group_cols)
        key_part = column_slice(key_rows, group_index, group_cols)
        value_part = column_slice(value_rows, group_index, group_cols)
        scores = (
            jnp.einsum("qhd,khd->hqk", query_part, key_part, preferred_element_type=jnp.float32)
            * head_scale
        )
        scores = jnp.where(allowed_back[None], scores, -jnp.inf)
        chances = jnp.exp(scores - head_pair(total_rims, group_index))
        grad_scores = jnp.einsum(
            "qhd,khd->hqk", grad_part, value_part, preferred_element_type=jnp.float32
        )
        slopes = (chances * (grad_scores - head_pair(delta_rims, group_index))).astype(jnp.bfloat16)
        grad_key = (
            jnp.einsum("hqk,qhd->khd", slopes, query_part, preferred_element_type=jnp.float32)
            * head_scale
        )
        grad_value = jnp.einsum(
            "hqk,qhd->khd",
            chances.astype(jnp.bfloat16),
            grad_part,
            preferred_element_type=jnp.float32,
        )
        return (
            grad_key.reshape(point_rows, group_cols).astype(jnp.bfloat16),
            grad_value.reshape(point_rows, group_cols).astype(jnp.bfloat16),
        )

    key_groups, value_groups = lax.map(key_group, group_list)
    grad_keys = jnp.transpose(key_groups, (1, 0, 2)).reshape(point_rows, D)
    grad_values = jnp.transpose(value_groups, (1, 0, 2)).reshape(point_rows, D)
    return (layer_out, grad_queries, grad_keys, grad_values, grad_weight)


def solution(mesh):
    return jax.shard_map(
        per_device,
        mesh=mesh,
        in_specs=(
            P("seq", None),
            P("seq", None),
            P("seq", None),
            P("seq"),
            P("seq", None),
            P(),
            P("seq"),
        ),
        out_specs=(P("seq", None), P("seq", None), P("seq", None), P("seq", None), P("seq")),
        check_vma=False,
    )
```

profile of v0, /device:TPU:8, one launch (start us, length us, event | category | flops | bytes accessed | tf_op | source)
XLA Modules:
  0.0 732.5 jit_solution(13220339848091693262)
XLA Ops:
  7.2 3.8 collective-permute-start.3
  13.0 3.0 collective-permute-done.3
  16.0 5.5 collective-permute-done
  26.0 3.6 collective-permute-start.1
  29.6 2.5 collective-permute-start.9
  37.0 5.4 collective-permute-start.21
  43.7 20.8 %collective-permute-start.18 = (f32[160]{0:T(256)S(1)}, f32[160]{0:T(256)S(1)}, u32[]{:S(2)}, u32[]{:S(2)}) collective-permute-start(f32[160]{0:T(256)S(1)} %get-tuple-element.493), channel_id=1, source_target_pairs={{0,1},{1,2},{2,3},{3,4},{4,5},{5,6},{6,7},{7,8},{8,9},{9,10},{10,1... | collective-permute-start | bytes 1928 | tf_op jit(solution)/shard_map/ppermute | solution.py:25
  67.3 2.4 collective-permute-start.12
  71.8 3.1 pad_maximum_fusion.1
  74.8 4.0 collective-permute-start.19
  78.8 3.4 collective-permute-start.2
  84.5 5.7 collective-permute-start.10
  92.2 2.6 collective-permute-start.20
  94.8 4.2 collective-permute-start.23
  100.2 25.9 %collective-permute-done.20 = f32[640]{0:T(1024)S(1)} collective-permute-done((f32[640]{0:T(1024)S(1)}, f32[640]{0:T(1024)S(1)}, u32[]{:S(2)}, u32[]{:S(2)}) %collective-permute-start.20) | collective-permute-done | bytes 2592 | tf_op jit(solution)/shard_map/ppermute | solution.py:25
  126.1 18.7 %collective-permute-start.16 = (bf16[320,1024]{1,0:T(8,128)(2,1)}, bf16[320,1024]{1,0:T(8,128)(2,1)S(1)}, u32[]{:S(2)}, u32[]{:S(2)}) collective-permute-start(bf16[320,1024]{1,0:T(8,128)(2,1)} %get-tuple-element.515), channel_id=1, source_target_pairs={{2,0},{3,1},{4,2},{5,3},{6,4},{7,5},{8,6},{9,7},{10,8},{11,9},{12,... | collective-permute-start | bytes 1966088 | tf_op jit(solution)/shard_map/ppermute | solution.py:25
  144.8 2.9 collective-permute-start.13
  150.8 3.3 pad_maximum_fusion.3
  154.1 3.9 collective-permute-start.8
  158.1 10.8 %collective-permute-done.16 = bf16[320,1024]{1,0:T(8,128)(2,1)S(1)} collective-permute-done((bf16[320,1024]{1,0:T(8,128)(2,1)}, bf16[320,1024]{1,0:T(8,128)(2,1)S(1)}, u32[]{:S(2)}, u32[]{:S(2)}) %collective-permute-start.16) | collective-permute-done | bytes 655392 | tf_op jit(solution)/shard_map/ppermute | solution.py:25
  170.8 3.2 collective-permute-done.13
  174.0 3.0 pad_maximum_fusion.5
  176.9 10.7 %collective-permute-start.14 = (bf16[640,1024]{1,0:T(8,128)(2,1)}, bf16[640,1024]{1,0:T(8,128)(2,1)}, u32[]{:S(2)}, u32[]{:S(2)}) collective-permute-start(bf16[640,1024]{1,0:T(8,128)(2,1)} %get-tuple-element.514), channel_id=1, source_target_pairs={{0,4},{1,5},{2,6},{3,7},{4,8},{5,9},{6,10},{7,11},{8,12},{9,13},{1... | collective-permute-start | bytes 3932168 | tf_op jit(solution)/shard_map/ppermute | solution.py:25
  189.7 2.5 constant_dynamic-update-slice_fusion.10
  198.4 51.3 %collective-permute-done.5 = bf16[640,1024]{1,0:T(8,128)(2,1)S(1)} collective-permute-done((bf16[640,1024]{1,0:T(8,128)(2,1)}, bf16[640,1024]{1,0:T(8,128)(2,1)S(1)}, u32[]{:S(2)}, u32[]{:S(2)}) %collective-permute-start.5) | collective-permute-done | bytes 1310752 | tf_op jit(solution)/shard_map/ppermute | solution.py:25
  251.0 7.5 %copy.114 = bf16[2400,1024]{0,1:T(8,128)(2,1)} copy(bf16[2400,1024]{1,0:T(8,128)(2,1)} %constant_dynamic-update-slice_fusion.4) | data formatting | bytes 9830400
  258.5 27.0 %collective-permute-done.8 = bf16[640,1024]{1,0:T(8,128)(2,1)} collective-permute-done((bf16[640,1024]{1,0:T(8,128)(2,1)}, bf16[640,1024]{1,0:T(8,128)(2,1)}, u32[]{:S(2)}, u32[]{:S(2)}) %collective-permute-start.8) | collective-permute-done | bytes 1310752 | tf_op jit(solution)/shard_map/ppermute | solution.py:25
  285.5 2.5 constant_dynamic-update-slice_fusion.17
  295.2 2.5 constant_dynamic-update-slice_fusion.11
  297.6 7.4 %copy.116 = bf16[2400,1024]{0,1:T(8,128)(2,1)} copy(bf16[2400,1024]{1,0:T(8,128)(2,1)} %constant_dynamic-update-slice_fusion.11) | data formatting | bytes 9830400
  305.1 49.3 %while.37 = (s32[]{:T(128)}, bf16[8,160,128]{1,2,0:T(8,128)(2,1)S(1)}, f32[8,2,160]{2,1,0:T(2,128)S(1)}, s32[8]{0:T(128)S(1)}, bf16[2400,1024]{0,1:T(8,128)(2,1)...) while((s32[]{:T(128)}, ...), condition=%wide.region_5.6_spmd.clone, body=%wide.region_2.5_spmd.clone.sunk | while | flops 203156160 | bytes 13989719 | solution.py:125
  356.3 2.4 collective-permute-start.24
  360.4 3.0 copy.150
  363.4 2.5 constant_dynamic-update-slice_fusion.24
  365.9 2.8 reshape.244
  368.7 3.0 convert_multiply_fusion
  371.8 5.1 collective-permute-start.33
  382.3 4.1 collective-permute-done.33
  386.4 7.8 %collective-permute-done.30 = bf16[160,1024]{1,0:T(8,128)(2,1)S(1)} collective-permute-done((bf16[160,1024]{1,0:T(8,128)(2,1)}, bf16[160,1024]{1,0:T(8,128)(2,1)S(1)}, u32[]{:S(2)}, u32[]{:S(2)}) %collective-permute-start.30) | collective-permute-done | bytes 327712 | tf_op jit(solution)/shard_map/ppermute | solution.py:25
  394.2 2.5 pad_maximum_fusion.15
  398.6 3.9 collective-permute-start.31
  402.6 3.7 collective-permute-start.28
  409.2 18.3 %collective-permute-done.28 = f32[320,16]{0,1:T(8,128)S(1)} collective-permute-done((f32[320,16]{0,1:T(8,128)S(1)}, f32[320,16]{0,1:T(8,128)S(1)}, u32[]{:S(2)}, u32[]{:S(2)}) %collective-permute-start.28) | collective-permute-done | bytes 20512 | tf_op jit(solution)/shard_map/ppermute | solution.py:25
  427.5 3.7 collective-permute-done.25
  434.1 5.0 collective-permute-start.29
  441.0 3.2 collective-permute-start.39
  446.1 2.5 constant_dynamic-update-slice_fusion.18
  454.4 3.9 collective-permute-start.37
  458.4 3.3 pad_maximum_fusion.7
  461.7 2.7 collective-permute-start.32
  464.5 4.0 collective-permute-start.35
  469.3 92.2 %while.38 = (s32[]{:T(128)}, bf16[8,160,128]{1,2,0:T(8,128)(2,1)}, s32[8]{0:T(128)S(1)}, bf16[2400,1024]{0,1:T(8,128)(2,1)}, bf16[160,1024]{0,1:T(8,128)(2,1)}, ...) while((s32[]{:T(128)}, bf16[8,160,128]{1,2,0:T(8,128)(2,1)}, ...), condition=%wide.region_8.9_spmd.clone, body=%wide.region_7.8_spmd.clone.sunk | while | flops 300712960 | bytes 11706793 | solution.py:166
  470.5 2.4 constant_dynamic-slice_fusion.20
  482.1 2.4 constant_dynamic-slice_fusion.20
  493.6 2.4 constant_dynamic-slice_fusion.20
  505.1 2.4 constant_dynamic-slice_fusion.20
  516.6 2.5 constant_dynamic-slice_fusion.20
  528.1 2.5 constant_dynamic-slice_fusion.20
  535.5 2.4 fusion.86
  539.7 2.4 constant_dynamic-slice_fusion.20
  551.2 2.4 constant_dynamic-slice_fusion.20
  564.4 4.8 collective-permute-start.41
  569.2 3.0 convolution_convert_fusion.1
  584.0 137.6 %while.39 = (s32[]{:T(128)}, bf16[8,160,128]{1,2,0:T(8,128)(2,1)}, bf16[8,160,128]{1,2,0:T(8,128)(2,1)}, s32[8]{0:T(128)S(1)}, bf16[2400,1024]{1,0:T(8,128)(2,1)...) while((s32[]{:T(128)}, bf16[8,160,128]{1,2,0:T(8,128)(2,1)}, ...), condition=%wide.region_10.11_spmd.clone, body=%wide.region_9.10_spmd.clone.sunk | while | flops 400189440 | bytes 18199064 | solution.py:209
  (416 shorter events, 320.7 us)
Async XLA Ops:
  7.2 352.5 %copy-start = (bf16[160,1024]{1,0:T(8,128)(2,1)S(1)}, bf16[160,1024]{1,0:T(8,128)(2,1)}, u32[]{:S(2)}) copy-start(bf16[160,1024]{1,0:T(8,128)(2,1)} %param.17) | copy-start | bytes 983044
  7.2 358.7 %all-gather.2.cloned.1.call-start = ((), (), s32[]{:S(2)}) async-start(), calls=%async_computation | async-start | bytes 2162688 | tf_op jit(solution)/shard_map/all_gather | solution.py:105
  7.2 8.8 %collective-permute-start.3 = (bf16[160,1024]{1,0:T(8,128)(2,1)}, bf16[160,1024]{1,0:T(8,128)(2,1)S(1)}, u32[]{:S(2)}, u32[]{:S(2)}) collective-permute-start(bf16[160,1024]{1,0:T(8,128)(2,1)} %param.15), channel_id=1, source_target_pairs={{1,0},{2,1},{3,2},{4,3},{5,4},{6,5},{7,6},{8,7},{9,8},{10,9},{11,1... | collective-permute-start | bytes 983048 | tf_op jit(solution)/shard_map/ppermute | solution.py:25
  11.0 10.4 %collective-permute-start = (bf16[160,1024]{1,0:T(8,128)(2,1)}, bf16[160,1024]{1,0:T(8,128)(2,1)S(1)}, u32[]{:S(2)}, u32[]{:S(2)}) collective-permute-start(bf16[160,1024]{1,0:T(8,128)(2,1)} %param.15), channel_id=1, source_target_pairs={{0,1},{1,2},{2,3},{3,4},{4,5},{5,6},{6,7},{7,8},{8,9},{9,10},{10,1... | collective-permute-start | bytes 983048 | tf_op jit(solution)/shard_map/ppermute | solution.py:25
  23.8 43.5 %collective-permute-start.4 = (bf16[320,1024]{1,0:T(8,128)(2,1)}, bf16[320,1024]{1,0:T(8,128)(2,1)S(1)}, u32[]{:S(2)}, u32[]{:S(2)}) collective-permute-start(bf16[320,1024]{1,0:T(8,128)(2,1)} %get-tuple-element.523), channel_id=1, source_target_pairs={{2,0},{3,1},{4,2},{5,3},{6,4},{7,5},{8,6},{9,7},{10,8},{11,9},{12,... | collective-permute-start | bytes 1966088 | tf_op jit(solution)/shard_map/ppermute | solution.py:25
  26.0 43.7 %collective-permute-start.1 = (bf16[320,1024]{1,0:T(8,128)(2,1)}, bf16[320,1024]{1,0:T(8,128)(2,1)}, u32[]{:S(2)}, u32[]{:S(2)}) collective-permute-start(bf16[320,1024]{1,0:T(8,128)(2,1)} %get-tuple-element.524), channel_id=1, source_target_pairs={{0,2},{1,3},{2,4},{3,5},{4,6},{5,7},{6,8},{7,9},{8,10},{9,11},{10,... | collective-permute-start | bytes 1966088 | tf_op jit(solution)/shard_map/ppermute | solution.py:25
  29.6 45.2 %collective-permute-start.9 = (bf16[160,1024]{1,0:T(8,128)(2,1)}, bf16[160,1024]{1,0:T(8,128)(2,1)S(1)}, u32[]{:S(2)}, u32[]{:S(2)}) collective-permute-start(bf16[160,1024]{1,0:T(8,128)(2,1)} %param.14), channel_id=1, source_target_pairs={{1,0},{2,1},{3,2},{4,3},{5,4},{6,5},{7,6},{8,7},{9,8},{10,9},{11,1... | collective-permute-start | bytes 983048 | tf_op jit(solution)/shard_map/ppermute | solution.py:25
  32.1 46.7 %collective-permute-start.6 = (bf16[160,1024]{1,0:T(8,128)(2,1)}, bf16[160,1024]{1,0:T(8,128)(2,1)S(1)}, u32[]{:S(2)}, u32[]{:S(2)}) collective-permute-start(bf16[160,1024]{1,0:T(8,128)(2,1)} %param.14), channel_id=1, source_target_pairs={{0,1},{1,2},{2,3},{3,4},{4,5},{5,6},{6,7},{7,8},{8,9},{9,10},{10,1... | collective-permute-start | bytes 983048 | tf_op jit(solution)/shard_map/ppermute | solution.py:25
  35.0 0.5 copy-start.18
  37.0 6.7 collective-permute-start.21
  43.7 21.6 %collective-permute-start.18 = (f32[160]{0:T(256)S(1)}, f32[160]{0:T(256)S(1)}, u32[]{:S(2)}, u32[]{:S(2)}) collective-permute-start(f32[160]{0:T(256)S(1)} %get-tuple-element.493), channel_id=1, source_target_pairs={{0,1},{1,2},{2,3},{3,4},{4,5},{5,6},{6,7},{7,8},{8,9},{9,10},{10,1... | collective-permute-start | bytes 1928 | tf_op jit(solution)/shard_map/ppermute | solution.py:25
  64.5 510.2 %all-reduce.3.cloned.1.call-start = ((), (), s32[]{:S(2)}) async-start(), calls=%async_computation.1 | async-start | bytes 8388608
  65.3 27.0 %collective-permute-start.15 = (bf16[160,1024]{1,0:T(8,128)(2,1)}, bf16[160,1024]{1,0:T(8,128)(2,1)S(1)}, u32[]{:S(2)}, u32[]{:S(2)}) collective-permute-start(bf16[160,1024]{1,0:T(8,128)(2,1)} %param.13), channel_id=1, source_target_pairs={{1,0},{2,1},{3,2},{4,3},{5,4},{6,5},{7,6},{8,7},{9,8},{10,9},{11,1... | collective-permute-start | bytes 983048 | tf_op jit(solution)/shard_map/ppermute | solution.py:25
  67.3 17.3 %copy-start.15 = (bf16[320,1024]{1,0:T(8,128)(2,1)}, bf16[320,1024]{1,0:T(8,128)(2,1)S(1)}, u32[]{:S(2)}) copy-start(bf16[320,1024]{1,0:T(8,128)(2,1)S(1)} %collective-permute-done.4) | copy-start | bytes 1966084
  67.3 27.5 %collective-permute-start.12 = (bf16[160,1024]{1,0:T(8,128)(2,1)}, bf16[160,1024]{1,0:T(8,128)(2,1)S(1)}, u32[]{:S(2)}, u32[]{:S(2)}) collective-permute-start(bf16[160,1024]{1,0:T(8,128)(2,1)} %param.13), channel_id=1, source_target_pairs={{0,1},{1,2},{2,3},{3,4},{4,5},{5,6},{6,7},{7,8},{8,9},{9,10},{10,1... | collective-permute-start | bytes 983048 | tf_op jit(solution)/shard_map/ppermute | solution.py:25
  69.7 29.3 %copy-start.4 = (bf16[160,1024]{1,0:T(8,128)(2,1)S(1)}, bf16[160,1024]{1,0:T(8,128)(2,1)}, u32[]{:S(2)}) copy-start(bf16[160,1024]{1,0:T(8,128)(2,1)} %param.13) | copy-start | bytes 983044
  69.7 14.8 %collective-permute-start.22 = (f32[320]{0:T(512)S(1)}, f32[320]{0:T(512)S(1)}, u32[]{:S(2)}, u32[]{:S(2)}) collective-permute-start(f32[320]{0:T(512)S(1)} %get-tuple-element.535), channel_id=1, source_target_pairs={{2,0},{3,1},{4,2},{5,3},{6,4},{7,5},{8,6},{9,7},{10,8},{11,9},{12,... | collective-permute-start | bytes 3848 | tf_op jit(solution)/shard_map/ppermute | solution.py:25
  74.8 15.4 %collective-permute-start.19 = (f32[320]{0:T(512)S(1)}, f32[320]{0:T(512)S(1)}, u32[]{:S(2)}, u32[]{:S(2)}) collective-permute-start(f32[320]{0:T(512)S(1)} %get-tuple-element.536), channel_id=1, source_target_pairs={{0,2},{1,3},{2,4},{3,5},{4,6},{5,7},{6,8},{7,9},{8,10},{9,11},{10,... | collective-permute-start | bytes 3848 | tf_op jit(solution)/shard_map/ppermute | solution.py:25
  78.8 108.8 %collective-permute-start.2 = (bf16[640,1024]{1,0:T(8,128)(2,1)}, bf16[640,1024]{1,0:T(8,128)(2,1)}, u32[]{:S(2)}, u32[]{:S(2)}) collective-permute-start(bf16[640,1024]{1,0:T(8,128)(2,1)} %get-tuple-element.522), channel_id=1, source_target_pairs={{0,4},{1,5},{2,6},{3,7},{4,8},{5,9},{6,10},{7,11},{8,12},{9,13},{1... | collective-permute-start | bytes 3932168 | tf_op jit(solution)/shard_map/ppermute | solution.py:25
  84.5 64.3 %collective-permute-start.10 = (bf16[320,1024]{1,0:T(8,128)(2,1)}, bf16[320,1024]{1,0:T(8,128)(2,1)}, u32[]{:S(2)}, u32[]{:S(2)}) collective-permute-start(bf16[320,1024]{1,0:T(8,128)(2,1)} %get-tuple-element.519), channel_id=1, source_target_pairs={{2,0},{3,1},{4,2},{5,3},{6,4},{7,5},{8,6},{9,7},{10,8},{11,9},{12,... | collective-permute-start | bytes 1966088 | tf_op jit(solution)/shard_map/ppermute | solution.py:25
  90.2 60.6 %collective-permute-start.7 = (bf16[320,1024]{1,0:T(8,128)(2,1)}, bf16[320,1024]{1,0:T(8,128)(2,1)}, u32[]{:S(2)}, u32[]{:S(2)}) collective-permute-start(bf16[320,1024]{1,0:T(8,128)(2,1)} %get-tuple-element.520), channel_id=1, source_target_pairs={{0,2},{1,3},{2,4},{3,5},{4,6},{5,7},{6,8},{7,9},{8,10},{9,11},{10,... | collective-permute-start | bytes 1966088 | tf_op jit(solution)/shard_map/ppermute | solution.py:25
  92.2 33.9 %collective-permute-start.20 = (f32[640]{0:T(1024)S(1)}, f32[640]{0:T(1024)S(1)}, u32[]{:S(2)}, u32[]{:S(2)}) collective-permute-start(f32[640]{0:T(1024)S(1)} %get-tuple-element.534), channel_id=1, source_target_pairs={{0,4},{1,5},{2,6},{3,7},{4,8},{5,9},{6,10},{7,11},{8,12},{9,13},{1... | collective-permute-start | bytes 7688 | tf_op jit(solution)/shard_map/ppermute | solution.py:25
  94.8 50.0 %collective-permute-start.23 = (f32[640]{0:T(1024)S(1)}, f32[640]{0:T(1024)S(1)}, u32[]{:S(2)}, u32[]{:S(2)}) collective-permute-start(f32[640]{0:T(1024)S(1)} %get-tuple-element.533), channel_id=1, source_target_pairs={{4,0},{5,1},{6,2},{7,3},{8,4},{9,5},{10,6},{11,7},{12,8},{13,9},{1... | collective-permute-start | bytes 7688 | tf_op jit(solution)/shard_map/ppermute | solution.py:25
  126.1 42.7 %collective-permute-start.16 = (bf16[320,1024]{1,0:T(8,128)(2,1)}, bf16[320,1024]{1,0:T(8,128)(2,1)S(1)}, u32[]{:S(2)}, u32[]{:S(2)}) collective-permute-start(bf16[320,1024]{1,0:T(8,128)(2,1)} %get-tuple-element.515), channel_id=1, source_target_pairs={{2,0},{3,1},{4,2},{5,3},{6,4},{7,5},{8,6},{9,7},{10,8},{11,9},{12,... | collective-permute-start | bytes 1966088 | tf_op jit(solution)/shard_map/ppermute | solution.py:25
  144.8 29.2 %collective-permute-start.13 = (bf16[320,1024]{1,0:T(8,128)(2,1)}, bf16[320,1024]{1,0:T(8,128)(2,1)}, u32[]{:S(2)}, u32[]{:S(2)}) collective-permute-start(bf16[320,1024]{1,0:T(8,128)(2,1)} %get-tuple-element.516), channel_id=1, source_target_pairs={{0,2},{1,3},{2,4},{3,5},{4,6},{5,7},{6,8},{7,9},{8,10},{9,11},{10,... | collective-permute-start | bytes 1966088 | tf_op jit(solution)/shard_map/ppermute | solution.py:25
  148.9 100.9 %collective-permute-start.5 = (bf16[640,1024]{1,0:T(8,128)(2,1)}, bf16[640,1024]{1,0:T(8,128)(2,1)S(1)}, u32[]{:S(2)}, u32[]{:S(2)}) collective-permute-start(bf16[640,1024]{1,0:T(8,128)(2,1)} %get-tuple-element.521), channel_id=1, source_target_pairs={{4,0},{5,1},{6,2},{7,3},{8,4},{9,5},{10,6},{11,7},{12,8},{13,9},{1... | collective-permute-start | bytes 3932168 | tf_op jit(solution)/shard_map/ppermute | solution.py:25
  154.1 131.4 %collective-permute-start.8 = (bf16[640,1024]{1,0:T(8,128)(2,1)}, bf16[640,1024]{1,0:T(8,128)(2,1)}, u32[]{:S(2)}, u32[]{:S(2)}) collective-permute-start(bf16[640,1024]{1,0:T(8,128)(2,1)} %get-tuple-element.518), channel_id=1, source_target_pairs={{0,4},{1,5},{2,6},{3,7},{4,8},{5,9},{6,10},{7,11},{8,12},{9,13},{1... | collective-permute-start | bytes 3932168 | tf_op jit(solution)/shard_map/ppermute | solution.py:25
  168.9 23.4 %copy-start.11 = (bf16[320,1024]{1,0:T(8,128)(2,1)}, bf16[320,1024]{1,0:T(8,128)(2,1)S(1)}, u32[]{:S(2)}) copy-start(bf16[320,1024]{1,0:T(8,128)(2,1)S(1)} %collective-permute-done.16) | copy-start | bytes 1966084
  168.9 126.3 %collective-permute-start.11 = (bf16[640,1024]{1,0:T(8,128)(2,1)}, bf16[640,1024]{1,0:T(8,128)(2,1)}, u32[]{:S(2)}, u32[]{:S(2)}) collective-permute-start(bf16[640,1024]{1,0:T(8,128)(2,1)} %get-tuple-element.517), channel_id=1, source_target_pairs={{4,0},{5,1},{6,2},{7,3},{8,4},{9,5},{10,6},{11,7},{12,8},{13,9},{1... | collective-permute-start | bytes 3932168 | tf_op jit(solution)/shard_map/ppermute | solution.py:25
  176.9 186.5 %collective-permute-start.14 = (bf16[640,1024]{1,0:T(8,128)(2,1)}, bf16[640,1024]{1,0:T(8,128)(2,1)}, u32[]{:S(2)}, u32[]{:S(2)}) collective-permute-start(bf16[640,1024]{1,0:T(8,128)(2,1)} %get-tuple-element.514), channel_id=1, source_target_pairs={{0,4},{1,5},{2,6},{3,7},{4,8},{5,9},{6,10},{7,11},{8,12},{9,13},{1... | collective-permute-start | bytes 3932168 | tf_op jit(solution)/shard_map/ppermute | solution.py:25
  187.7 9.9 %copy-start.16 = (bf16[320,1024]{1,0:T(8,128)(2,1)S(1)}, bf16[320,1024]{1,0:T(8,128)(2,1)}, u32[]{:S(2)}) copy-start(bf16[320,1024]{1,0:T(8,128)(2,1)} %copy-done.15) | copy-start | bytes 1966084
  187.7 253.3 %collective-permute-start.17 = (bf16[640,1024]{1,0:T(8,128)(2,1)}, bf16[640,1024]{1,0:T(8,128)(2,1)}, u32[]{:S(2)}, u32[]{:S(2)}) collective-permute-start(bf16[640,1024]{1,0:T(8,128)(2,1)} %get-tuple-element.513), channel_id=1, source_target_pairs={{4,0},{5,1},{6,2},{7,3},{8,4},{9,5},{10,6},{11,7},{12,8},{13,9},{1... | collective-permute-start | bytes 3932168 | tf_op jit(solution)/shard_map/ppermute | solution.py:25
  354.4 6.0 copy-start.3
  354.4 48.1 %collective-permute-start.27 = (f32[160,16]{0,1:T(8,128)S(1)}, f32[160,16]{0,1:T(8,128)S(1)}, u32[]{:S(2)}, u32[]{:S(2)}) collective-permute-start(f32[160,16]{0,1:T(8,128)S(1)} %bitcast.174), channel_id=1, source_target_pairs={{1,0},{2,1},{3,2},{4,3},{5,4},{6,5},{7,6},{8,7},{9,8},{10,9},{11,1... | collective-permute-start | bytes 30728 | tf_op jit(solution)/shard_map/ppermute | solution.py:25
  356.3 46.2 %collective-permute-start.24 = (f32[160,16]{0,1:T(8,128)S(1)}, f32[160,16]{0,1:T(8,128)S(1)}, u32[]{:S(2)}, u32[]{:S(2)}) collective-permute-start(f32[160,16]{0,1:T(8,128)S(1)} %bitcast.175), channel_id=1, source_target_pairs={{0,1},{1,2},{2,3},{3,4},{4,5},{5,6},{6,7},{7,8},{8,9},{9,10},{10,1... | collective-permute-start | bytes 30728 | tf_op jit(solution)/shard_map/ppermute | solution.py:25
  368.7 12.9 %copy-start.2 = (bf16[1024,1024]{1,0:T(8,128)(2,1)}, bf16[1024,1024]{1,0:T(8,128)(2,1)S(1)}, u32[]{:S(2)}) copy-start(bf16[1024,1024]{1,0:T(8,128)(2,1)S(1)} %reshape.244) | copy-start | bytes 6291460
  371.8 61.5 %copy-start.12 = (bf16[320,1024]{1,0:T(8,128)(2,1)S(1)}, bf16[320,1024]{1,0:T(8,128)(2,1)}, u32[]{:S(2)}) copy-start(bf16[320,1024]{1,0:T(8,128)(2,1)} %copy-done.11) | copy-start | bytes 1966084
  371.8 14.7 %collective-permute-start.33 = (bf16[160,1024]{1,0:T(8,128)(2,1)}, bf16[160,1024]{1,0:T(8,128)(2,1)S(1)}, u32[]{:S(2)}, u32[]{:S(2)}) collective-permute-start(bf16[160,1024]{1,0:T(8,128)(2,1)} %get-tuple-element.838), channel_id=1, source_target_pairs={{1,0},{2,1},{3,2},{4,3},{5,4},{6,5},{7,6},{8,7},{9,8},{10,9},{11,1... | collective-permute-start | bytes 983048 | tf_op jit(solution)/shard_map/ppermute | solution.py:25
  376.9 17.4 %collective-permute-start.30 = (bf16[160,1024]{1,0:T(8,128)(2,1)}, bf16[160,1024]{1,0:T(8,128)(2,1)S(1)}, u32[]{:S(2)}, u32[]{:S(2)}) collective-permute-start(bf16[160,1024]{1,0:T(8,128)(2,1)} %get-tuple-element.838), channel_id=1, source_target_pairs={{0,1},{1,2},{2,3},{3,4},{4,5},{5,6},{6,7},{7,8},{8,9},{9,10},{10,1... | collective-permute-start | bytes 983048 | tf_op jit(solution)/shard_map/ppermute | solution.py:25
  386.4 72.0 %copy-start.6 = (bf16[160,1024]{1,0:T(8,128)(2,1)}, bf16[160,1024]{1,0:T(8,128)(2,1)S(1)}, u32[]{:S(2)}) copy-start(bf16[160,1024]{1,0:T(8,128)(2,1)S(1)} %collective-permute-done.33) | copy-start | bytes 983044
  394.2 44.9 %copy-start.8 = (bf16[160,1024]{1,0:T(8,128)(2,1)}, bf16[160,1024]{1,0:T(8,128)(2,1)S(1)}, u32[]{:S(2)}) copy-start(bf16[160,1024]{1,0:T(8,128)(2,1)S(1)} %collective-permute-done.30) | copy-start | bytes 983044
  396.7 61.7 %collective-permute-start.34 = (bf16[320,1024]{1,0:T(8,128)(2,1)}, bf16[320,1024]{1,0:T(8,128)(2,1)S(1)}, u32[]{:S(2)}, u32[]{:S(2)}) collective-permute-start(bf16[320,1024]{1,0:T(8,128)(2,1)} %get-tuple-element.511), channel_id=1, source_target_pairs={{2,0},{3,1},{4,2},{5,3},{6,4},{7,5},{8,6},{9,7},{10,8},{11,9},{12,... | collective-permute-start | bytes 1966088 | tf_op jit(solution)/shard_map/ppermute | solution.py:25
  398.6 59.8 %collective-permute-start.31 = (bf16[320,1024]{1,0:T(8,128)(2,1)}, bf16[320,1024]{1,0:T(8,128)(2,1)}, u32[]{:S(2)}, u32[]{:S(2)}) collective-permute-start(bf16[320,1024]{1,0:T(8,128)(2,1)} %get-tuple-element.512), channel_id=1, source_target_pairs={{0,2},{1,3},{2,4},{3,5},{4,6},{5,7},{6,8},{7,9},{8,10},{9,11},{10,... | collective-permute-start | bytes 1966088 | tf_op jit(solution)/shard_map/ppermute | solution.py:25
  402.6 24.9 %collective-permute-start.28 = (f32[320,16]{0,1:T(8,128)S(1)}, f32[320,16]{0,1:T(8,128)S(1)}, u32[]{:S(2)}, u32[]{:S(2)}) collective-permute-start(f32[320,16]{0,1:T(8,128)S(1)} %get-tuple-element.531), channel_id=1, source_target_pairs={{2,0},{3,1},{4,2},{5,3},{6,4},{7,5},{8,6},{9,7},{10,8},{11,9},{12,... | collective-permute-start | bytes 61448 | tf_op jit(solution)/shard_map/ppermute | solution.py:25
  406.3 24.9 %collective-permute-start.25 = (f32[320,16]{0,1:T(8,128)S(1)}, f32[320,16]{0,1:T(8,128)S(1)}, u32[]{:S(2)}, u32[]{:S(2)}) collective-permute-start(f32[320,16]{0,1:T(8,128)S(1)} %get-tuple-element.532), channel_id=1, source_target_pairs={{0,2},{1,3},{2,4},{3,5},{4,6},{5,7},{6,8},{7,9},{8,10},{9,11},{10,... | collective-permute-start | bytes 61448 | tf_op jit(solution)/shard_map/ppermute | solution.py:25
  431.3 12.9 %collective-permute-start.26 = (f32[640,16]{0,1:T(8,128)S(1)}, f32[640,16]{0,1:T(8,128)S(1)}, u32[]{:S(2)}, u32[]{:S(2)}) collective-permute-start(f32[640,16]{0,1:T(8,128)S(1)} %get-tuple-element.530), channel_id=1, source_target_pairs={{0,4},{1,5},{2,6},{3,7},{4,8},{5,9},{6,10},{7,11},{8,12},{9,13},{1... | collective-permute-start | bytes 122888 | tf_op jit(solution)/shard_map/ppermute | solution.py:25
  434.1 14.5 %collective-permute-start.29 = (f32[640,16]{0,1:T(8,128)S(1)}, f32[640,16]{0,1:T(8,128)S(1)}, u32[]{:S(2)}, u32[]{:S(2)}) collective-permute-start(f32[640,16]{0,1:T(8,128)S(1)} %get-tuple-element.529), channel_id=1, source_target_pairs={{4,0},{5,1},{6,2},{7,3},{8,4},{9,5},{10,6},{11,7},{12,8},{13,9},{1... | collective-permute-start | bytes 122888 | tf_op jit(solution)/shard_map/ppermute | solution.py:25
  440.6 17.9 %copy-start.9 = (bf16[160,1024]{1,0:T(8,128)(2,1)S(1)}, bf16[160,1024]{1,0:T(8,128)(2,1)}, u32[]{:S(2)}) copy-start(bf16[160,1024]{1,0:T(8,128)(2,1)} %copy-done.8) | copy-start | bytes 983044
  441.0 8.4 %collective-permute-start.39 = (f32[160,16]{1,0:T(8,128)S(1)}, f32[160,16]{1,0:T(8,128)S(1)}, u32[]{:S(2)}, u32[]{:S(2)}) collective-permute-start(f32[160,16]{1,0:T(8,128)S(1)} %reduce_sum.28), channel_id=1, source_target_pairs={{1,0},{2,1},{3,2},{4,3},{5,4},{6,5},{7,6},{8,7},{9,8},{10,9},{11,1... | collective-permute-start | bytes 30728 | tf_op jit(solution)/shard_map/ppermute | solution.py:25
  444.2 7.6 %collective-permute-start.36 = (f32[160,16]{1,0:T(8,128)S(1)}, f32[160,16]{1,0:T(8,128)S(1)}, u32[]{:S(2)}, u32[]{:S(2)}) collective-permute-start(f32[160,16]{1,0:T(8,128)S(1)} %reduce_sum.28), channel_id=1, source_target_pairs={{0,1},{1,2},{2,3},{3,4},{4,5},{5,6},{6,7},{7,8},{8,9},{9,10},{10,1... | collective-permute-start | bytes 30728 | tf_op jit(solution)/shard_map/ppermute | solution.py:25
  452.5 109.0 %collective-permute-start.40 = (f32[320,16]{0,1:T(8,128)}, f32[320,16]{0,1:T(8,128)}, u32[]{:S(2)}, u32[]{:S(2)}) collective-permute-start(f32[320,16]{0,1:T(8,128)} %get-tuple-element.527), channel_id=1, source_target_pairs={{2,0},{3,1},{4,2},{5,3},{6,4},{7,5},{8,6},{9,7},{10,8},{11,9},{12,... | collective-permute-start | bytes 61448 | tf_op jit(solution)/shard_map/ppermute | solution.py:25
  454.4 107.1 %collective-permute-start.37 = (f32[320,16]{0,1:T(8,128)}, f32[320,16]{0,1:T(8,128)}, u32[]{:S(2)}, u32[]{:S(2)}) collective-permute-start(f32[320,16]{0,1:T(8,128)} %get-tuple-element.528), channel_id=1, source_target_pairs={{0,2},{1,3},{2,4},{3,5},{4,6},{5,7},{6,8},{7,9},{8,10},{9,11},{10,... | collective-permute-start | bytes 61448 | tf_op jit(solution)/shard_map/ppermute | solution.py:25
  458.4 10.9 %copy-start.13 = (bf16[320,1024]{1,0:T(8,128)(2,1)}, bf16[320,1024]{1,0:T(8,128)(2,1)S(1)}, u32[]{:S(2)}) copy-start(bf16[320,1024]{1,0:T(8,128)(2,1)S(1)} %collective-permute-done.34) | copy-start | bytes 1966084
  461.7 114.5 %collective-permute-start.32 = (bf16[640,1024]{1,0:T(8,128)(2,1)}, bf16[640,1024]{1,0:T(8,128)(2,1)}, u32[]{:S(2)}, u32[]{:S(2)}) collective-permute-start(bf16[640,1024]{1,0:T(8,128)(2,1)} %get-tuple-element.510), channel_id=1, source_target_pairs={{0,4},{1,5},{2,6},{3,7},{4,8},{5,9},{6,10},{7,11},{8,12},{9,13},{1... | collective-permute-start | bytes 3932168 | tf_op jit(solution)/shard_map/ppermute | solution.py:25
  464.5 115.6 %collective-permute-start.35 = (bf16[640,1024]{1,0:T(8,128)(2,1)}, bf16[640,1024]{1,0:T(8,128)(2,1)}, u32[]{:S(2)}, u32[]{:S(2)}) collective-permute-start(bf16[640,1024]{1,0:T(8,128)(2,1)} %get-tuple-element.509), channel_id=1, source_target_pairs={{4,0},{5,1},{6,2},{7,3},{8,4},{9,5},{10,6},{11,7},{12,8},{13,9},{1... | collective-permute-start | bytes 3932168 | tf_op jit(solution)/shard_map/ppermute | solution.py:25
  561.5 10.7 %copy-start.17 = (bf16[8,160,128]{1,2,0:T(8,128)(2,1)S(1)}, bf16[8,160,128]{1,2,0:T(8,128)(2,1)}, u32[]{:S(2)}) copy-start(bf16[8,160,128]{1,2,0:T(8,128)(2,1)} %get-tuple-element.160) | copy-start | bytes 983044
  562.4 10.7 %collective-permute-start.38 = (f32[640,16]{0,1:T(8,128)S(1)}, f32[640,16]{0,1:T(8,128)S(1)}, u32[]{:S(2)}, u32[]{:S(2)}) collective-permute-start(f32[640,16]{0,1:T(8,128)S(1)} %get-tuple-element.526), channel_id=1, source_target_pairs={{0,4},{1,5},{2,6},{3,7},{4,8},{5,9},{6,10},{7,11},{8,12},{9,13},{1... | collective-permute-start | bytes 122888 | tf_op jit(solution)/shard_map/ppermute | solution.py:25
  564.4 8.8 %collective-permute-start.41 = (f32[640,16]{0,1:T(8,128)S(1)}, f32[640,16]{0,1:T(8,128)S(1)}, u32[]{:S(2)}, u32[]{:S(2)}) collective-permute-start(f32[640,16]{0,1:T(8,128)S(1)} %get-tuple-element.525), channel_id=1, source_target_pairs={{4,0},{5,1},{6,2},{7,3},{8,4},{9,5},{10,6},{11,7},{12,8},{13,9},{1... | collective-permute-start | bytes 122888 | tf_op jit(solution)/shard_map/ppermute | solution.py:25
  572.2 6.6 copy-start.10
  576.2 3.7 copy-start.7
  576.2 3.7 copy-start.14
  579.9 4.1 copy-start.19
  581.4 2.6 copy-start.5
  721.7 3.9 copy-start.1
Sparse Core Ops, SparseCore 0:
  64.6 92.3 all-gather.1
  363.5 182.6 all-reduce.2
where the time goes:
time: 740 us; the launch traced here: 732 us
  local copies, waits for them, and re-layouts  215 us (29%)
  starting transfers between devices  167 us (23%)
  waiting for transfers between devices  165 us (22%)
  matrix products  104 us (14%)
  other arithmetic  39.8 us (5%)
  loops' own time  26.8 us (4%)
  between operations  14.9 us (2%)
    ppermute x42, starting transfers between devices, passed_along(): return lax.ppermute(block, axis, route)  167 us
    ppermute x42, waiting for transfers between devices, passed_along(): return lax.ppermute(block, axis, route)  165 us
    dynamic_slice x96, local copies, waits for them, and re-layouts, column_slice(): lax.dynamic_slice_in_dim(block, group_index * group_cols, group_cols, 1)  103 us
    unnamed x70, local copies, waits for them, and re-layouts  51.2 us
    concatenate x14, other arithmetic, join_rows(): return jax.tree.map(lambda *blocks: jnp.concatenate(blocks, 0), *pieces)  22.8 us
    dot_general x8, matrix products, query_group(): jnp.einsum('hqk,khd->qhd', slopes, key_part, preferred_element_type=jnp.f...  18.9 us
    dot_general x8, matrix products, key_group(): jnp.einsum('hqk,qhd->khd', slopes, query_part, preferred_element_type=jnp...  18.8 us
    dot_general x8, matrix products, key_group(): jnp.einsum('qhd,khd->hqk', query_part, key_part, preferred_element_type=j...  16.4 us
  transfers between devices with their start and end apart: 44, of which 14 were waited for; matrix products, arithmetic and copies ran while one was open for 30% of the time, Pallas kernels for 0%

commit v1 on v0

v1 whole, which is shorter than its diff:
```python
import functools
import math

import jax
import jax.numpy as jnp
from jax import lax
from jax.experimental import pallas as pl
from jax.experimental.pallas import tpu as pltpu
from jax.sharding import PartitionSpec as P

HEAD = 64
WIN = 1120
PAIR = 2 * HEAD
QBLOCK = 256
CHUNK = 256
LANES = 128
SUB = 16
DIGIT = 32
VMEM_LIMIT = 60 * 1024 * 1024


def up(value, step):
    return (value + step - 1) // step * step


def whole(shape):
    return pl.BlockSpec(shape, lambda *_: (0,) * len(shape))


def nt_dot(a, b):
    return lax.dot_general(a, b, (((1,), (1,)), ((), ())), preferred_element_type=jnp.float32)


def nn_dot(a, b):
    return lax.dot_general(a, b, (((1,), (0,)), ((), ())), preferred_element_type=jnp.float32)


def call(kernel, out_shape, flops=0, moved=0, exps=0, **kwargs):
    return pl.pallas_call(
        kernel,
        out_shape=out_shape,
        compiler_params=pltpu.CompilerParams(vmem_limit_bytes=VMEM_LIMIT),
        cost_estimate=pl.CostEstimate(flops=flops, bytes_accessed=moved, transcendentals=exps),
        **kwargs,
    )


def pack_kernel(points, q_ref, k_ref, v_ref, extra_ref, x_ref):
    for peer in range(x_ref.shape[0]):
        cols = slice(peer * PAIR, (peer + 1) * PAIR)
        x_ref[peer, 0:points, :] = q_ref[:, cols]
        x_ref[peer, points:2 * points, :] = k_ref[:, cols]
        x_ref[peer, 2 * points:3 * points, :] = v_ref[:, cols]
        x_ref[peer, 3 * points:, :] = extra_ref[...]


def block_range(start_row):
    low = jnp.min(start_row) // LANES * LANES
    high = jnp.max(start_row) + WIN
    return pl.multiple_of(low, LANES), (high - low + CHUNK - 1) // CHUNK


def head_rows(block, head):
    lane = lax.broadcasted_iota(jnp.int32, block.shape, 1)
    keep = (lane >= head * HEAD) & (lane < (head + 1) * HEAD)
    return jnp.where(keep, block, jnp.zeros_like(block))


def forward_kernel(
    points, reach, offset,
    x_ref, low_ref, high_ref, start_ref,
    p_ref, mixt_ref, mix_ref, inv_ref, q_ref, k_ref, v_ref, kt_ref,
    s_ref, vt_ref, acc_ref,
):
    group = x_ref.shape[0]
    total = k_ref.shape[0]

    @pl.when(pl.program_id(0) == 0)
    def _():
        for ref, base in ((k_ref, 0), (v_ref, points)):
            row = offset - reach * points
            if row:
                ref[0:row, :] = jnp.zeros((row, PAIR), ref.dtype)
            for j in range(reach):
                ref[row:row + points, :] = low_ref[j, base:base + points, :]
                row += points
            for j in range(group):
                ref[row:row + points, :] = x_ref[j, points + base:2 * points + base, :]
                row += points
            for j in range(reach):
                ref[row:row + points, :] = high_ref[j, base:base + points, :]
                row += points
            ref[row:, :] = jnp.zeros((total - row, PAIR), ref.dtype)
        for j in range(group):
            q_ref[j * points:(j + 1) * points, :] = x_ref[j, 0:points, :] * (1.0 / math.sqrt(HEAD))
        for t in range(total // LANES):
            rows = slice(t * LANES, (t + 1) * LANES)
            kt_ref[:, rows] = k_ref[rows, :].T
            vt_ref[:, rows] = v_ref[rows, :].T

    block = pl.program_id(0)
    start_row = start_ref[...]
    low, chunks = block_range(start_row)
    q_block = q_ref[pl.ds(pl.multiple_of(block * QBLOCK, QBLOCK), QBLOCK), :]
    q_heads = [head_rows(q_block, h) for h in range(2)]
    key_row = lax.broadcasted_iota(jnp.int32, (CHUNK, QBLOCK), 0) - start_row

    def score_chunk(c, tops):
        base = pl.multiple_of(low + c * CHUNK, LANES)
        keys = k_ref[pl.ds(base, CHUNK), :]
        spot = key_row + base
        valid = (spot >= 0) & (spot < WIN)
        result = []
        for h in range(2):
            scores = jnp.where(valid, nt_dot(keys, q_heads[h]), -jnp.inf)
            s_ref[h, pl.ds(pl.multiple_of(c * CHUNK, CHUNK), CHUNK), :] = scores
            result.append(jnp.maximum(tops[h], jnp.max(scores.reshape(CHUNK // 8, 8, QBLOCK), axis=0)))
        return tuple(result)

    empty = jnp.full((8, QBLOCK), -jnp.inf, jnp.float32)
    tops = lax.fori_loop(0, chunks, score_chunk, (empty, empty))
    tops = [jnp.max(top, axis=0, keepdims=True) for top in tops]
    acc_ref[...] = jnp.zeros_like(acc_ref)

    def mix_chunk(c, sums):
        base = pl.multiple_of(low + c * CHUNK, LANES)
        rows = pl.ds(pl.multiple_of(c * CHUNK, CHUNK), CHUNK)
        result = []
        for h in range(2):
            weights = jnp.exp(s_ref[h, rows, :] - tops[h])
            rounded = weights.astype(jnp.bfloat16)
            p_ref[0, h, rows, :] = rounded
            acc_ref[h] += nn_dot(vt_ref[h * HEAD:(h + 1) * HEAD, pl.ds(base, CHUNK)], rounded)
            result.append(sums[h] + jnp.sum(weights.reshape(CHUNK // 8, 8, QBLOCK), axis=0))
        return tuple(result)

    none = jnp.zeros((8, QBLOCK), jnp.float32)
    sums = lax.fori_loop(0, chunks, mix_chunk, (none, none))
    inverse = [1.0 / jnp.sum(part, axis=0, keepdims=True) for part in sums]
    mixed = jnp.concatenate([acc_ref[h] * inverse[h] for h in range(2)], axis=0)
    mixt_ref[...] = mixed.astype(jnp.bfloat16)
    mix_ref[...] = mixed.T.astype(jnp.bfloat16)
    inv_ref[...] = jnp.concatenate([jnp.broadcast_to(part, (4, QBLOCK)) for part in inverse], axis=0)


def backward_kernel(
    points, reach, offset, scale,
    place_ref, start_ref, p_ref, mixt_ref, inv_ref, q_ref, k_ref, v_ref, kt_ref, w_ref, *rest,
):
    group = (q_ref.shape[0]) // points
    cot_refs = rest[:group]
    dq_ref, low_ref, high_ref, own_ref, gw_ref, cot_ref, dk_ref, dv_ref, acc_ref = rest[group:]
    block = pl.program_id(0)
    rows = pl.ds(pl.multiple_of(block * QBLOCK, QBLOCK), QBLOCK)

    @pl.when(block == 0)
    def _():
        place = place_ref[0]
        for j in range(group):
            spot = pl.multiple_of((place ^ j) * points, SUB)
            cot_ref[pl.ds(spot, points), :] = cot_refs[j][...]
        dk_ref[...] = jnp.zeros_like(dk_ref)
        dv_ref[...] = jnp.zeros_like(dv_ref)
        gw_ref[...] = jnp.zeros_like(gw_ref)

    low, chunks = block_range(start_ref[...])
    cot_block = cot_ref[rows, :]
    gw_ref[...] += nn_dot(mixt_ref[...], cot_block) * scale
    grad = nt_dot(w_ref[...], cot_block).astype(jnp.bfloat16).astype(jnp.float32)
    q_block = q_ref[rows, :]
    row_id = lax.broadcasted_iota(jnp.int32, (PAIR, QBLOCK), 0)
    grads_t, grads, deltas, q_heads = [], [], [], []
    for h in range(2):
        keep = (row_id >= h * HEAD) & (row_id < (h + 1) * HEAD)
        part = jnp.where(keep, grad * inv_ref[4 * h:4 * h + 1, :], 0.0)
        rounded = part.astype(jnp.bfloat16)
        part = rounded.astype(jnp.float32)
        deltas.append(jnp.sum(part * mixt_ref[...].astype(jnp.float32), axis=0, keepdims=True))
        grads_t.append(rounded)
        grads.append(part.T.astype(jnp.bfloat16))
        q_heads.append(head_rows(q_block, h))
    acc_ref[...] = jnp.zeros_like(acc_ref)

    def chunk_step(c, carry):
        base = pl.multiple_of(low + c * CHUNK, LANES)
        spot = pl.ds(base, CHUNK)
        part = pl.ds(pl.multiple_of(c * CHUNK, CHUNK), CHUNK)
        values = v_ref[spot, :]
        dk, dv = dk_ref[spot, :], dv_ref[spot, :]
        for h in range(2):
            chance = p_ref[0, h, part, :]
            slope = nn_dot(values, grads_t[h]) - deltas[h]
            slope = (chance.astype(jnp.float32) * slope).astype(jnp.bfloat16)
            acc_ref[h] += nn_dot(kt_ref[h * HEAD:(h + 1) * HEAD, spot], slope)
            dk += nn_dot(slope, q_heads[h])
            dv += nn_dot(chance, grads[h])
        dk_ref[spot, :] = dk
        dv_ref[spot, :] = dv
        return carry

    lax.fori_loop(0, chunks, chunk_step, 0)
    grad_q = jnp.concatenate([acc_ref[h] for h in range(2)], axis=0) * (1.0 / math.sqrt(HEAD))
    dq_ref[...] = grad_q.T.astype(jnp.bfloat16)

    @pl.when(block == pl.num_programs(0) - 1)
    def _():
        for ref, base in ((dk_ref, 0), (dv_ref, points)):
            row = offset - reach * points
            for j in range(reach):
                low_ref[j, base:base + points, :] = ref[row:row + points, :].astype(jnp.bfloat16)
                row += points
            for j in range(group):
                own_ref[j, base:base + points, :] = ref[row:row + points, :]
                row += points
            for j in range(reach):
                high_ref[j, base:base + points, :] = ref[row:row + points, :].astype(jnp.bfloat16)
                row += points


def add_kernel(own_ref, below_ref, above_ref, out_ref):
    group, reach = own_ref.shape[0], below_ref.shape[0]
    for j in range(group):
        value = own_ref[j]
        if j < reach:
            value += below_ref[j].astype(jnp.float32)
        if j >= group - reach:
            value += above_ref[j - (group - reach)].astype(jnp.float32)
        out_ref[j] = value.astype(jnp.bfloat16)


def layer_kernel(points, place_ref, y_ref, *rest):
    group = y_ref.shape[0]
    w_refs = rest[:group]
    layer_ref, dq_ref = rest[group:]
    place = place_ref[0]
    total = nn_dot(y_ref[place, 0:points, :], w_refs[0][...])
    for j in range(1, group):
        total += nn_dot(y_ref[place ^ j, 0:points, :], w_refs[j][...])
    layer_ref[...] = total.astype(jnp.bfloat16)
    for j in range(group):
        dq_ref[:, j * PAIR:(j + 1) * PAIR] = y_ref[j, points:, :]


def split_kernel(points, y_ref, dk_ref, dv_ref):
    for j in range(y_ref.shape[0]):
        cols = slice(j * PAIR, (j + 1) * PAIR)
        dk_ref[:, cols] = y_ref[j, 0:points, :]
        dv_ref[:, cols] = y_ref[j, points:, :]


def permute(block, move):
    devices = range(lax.axis_size("seq"))
    return lax.ppermute(block, "seq", [(i, move(i)) for i in devices if move(i) in devices])


def gather_group(block, group):
    pieces = {0: block}
    for j in range(2, group, 2):
        pieces[j] = permute(block, lambda i, j=j: i ^ j)
    for j in range(0, group, 2):
        pieces[j + 1] = permute(pieces[j], lambda i: i ^ 1)
    return [pieces[j] for j in range(group)]


def per_device(queries, key_rows, value_rows, out_weight, cotangent, row_lengths, window_shift):
    points, width = queries.shape
    devices = lax.axis_size("seq")
    group = width // PAIR
    planes = devices // group
    all_points = points * devices
    plane_points = points * group
    reach = (WIN - 2 + points) // points
    offset = up(reach * points, LANES)
    span = 2 * offset + QBLOCK
    blocks = plane_points // QBLOCK
    total = up((blocks - 1) * QBLOCK + span + LANES, LANES)
    device = lax.axis_index("seq")
    plane, place = device // group, device % group
    place_list = place.reshape(1)
    groups = [[g * group + p for p in range(group)] for g in range(planes)]
    bf16, f32 = jnp.bfloat16, jnp.float32

    def shape(dims, kind=bf16):
        return jax.ShapeDtypeStruct(dims, kind)

    extra_rows = up(-(-2 * points // PAIR), SUB)
    digits = jnp.concatenate([window_shift // DIGIT, window_shift % DIGIT]).astype(bf16)
    extra = jnp.pad(digits, (0, extra_rows * PAIR - 2 * points)).reshape(extra_rows, PAIR)
    rows = 3 * points + extra_rows
    packed = call(
        functools.partial(pack_kernel, points), shape((group, rows, PAIR)),
        moved=12 * points * width,
    )(queries, key_rows, value_rows, extra)

    weight = out_weight.reshape(-1, width)
    part_rows = weight.shape[0]
    got = []
    for s in range(planes):
        got.append(permute(weight, lambda i, s=s: (i % planes + s) % planes * group + i // planes))
    order = jnp.stack(got[::-1] + got[::-1])
    own_weight = lax.dynamic_slice_in_dim(order, planes - 1 - plane, planes, 0).reshape(planes * part_rows, width)
    cots = gather_group(cotangent, group)

    swapped = lax.all_to_all(packed, "seq", 0, 0, tiled=True, axis_index_groups=groups)
    low_halo = permute(swapped[group - reach:, points:3 * points], lambda i: i + group)
    high_halo = permute(swapped[:reach, points:3 * points], lambda i: i - group)

    point_index = plane * plane_points + jnp.arange(plane_points, dtype=jnp.int32)
    passed = jnp.cumsum(row_lengths)[None, :] <= point_index[:, None]
    row_first = jnp.sum(jnp.where(passed, row_lengths[None, :], 0), axis=1)
    codes = swapped[:, 3 * points:].reshape(group, extra_rows * PAIR).astype(jnp.int32)
    shifts = (codes[:, :points] * DIGIT + codes[:, points:2 * points]).reshape(plane_points)
    starts = jnp.clip(row_first - shifts, 0, all_points - WIN) - plane * plane_points + offset
    starts = starts.reshape(1, plane_points)

    start_spec = pl.BlockSpec((1, QBLOCK), lambda b, *_: (0, b))
    chance_spec = pl.BlockSpec((1, 2, span, QBLOCK), lambda b, *_: (b, 0, 0, 0))
    column_spec = pl.BlockSpec((PAIR, QBLOCK), lambda b, *_: (0, b))
    row_spec = pl.BlockSpec((QBLOCK, PAIR), lambda b, *_: (b, 0))
    inverse_spec = pl.BlockSpec((8, QBLOCK), lambda b, *_: (0, b))
    work = 2 * 2 * plane_points * span * HEAD
    chances, mixed_t, mixed, inverse, q_all, k_all, v_all, kt_all = call(
        functools.partial(forward_kernel, points, reach, offset),
        (
            shape((blocks, 2, span, QBLOCK)), shape((PAIR, plane_points)), shape((plane_points, PAIR)),
            shape((8, plane_points), f32), shape((plane_points, PAIR)), shape((total, PAIR)),
            shape((total, PAIR)), shape((PAIR, total)),
        ),
        flops=8 * work, moved=40 * plane_points * PAIR, exps=2 * plane_points * span,
        grid=(blocks,),
        in_specs=[whole(swapped.shape), whole(low_halo.shape), whole(high_halo.shape), start_spec],
        out_specs=(
            chance_spec, column_spec, row_spec, inverse_spec, whole((plane_points, PAIR)),
            whole((total, PAIR)), whole((total, PAIR)), whole((PAIR, total)),
        ),
        scratch_shapes=[
            pltpu.VMEM((2, span, QBLOCK), f32), pltpu.VMEM((PAIR, total), bf16),
            pltpu.VMEM((2, HEAD, QBLOCK), f32),
        ],
    )(swapped, low_halo, high_halo, starts)

    weights = gather_group(own_weight, group)
    grad_q, low_part, high_part, own_part, weight_part = call(
        functools.partial(backward_kernel, points, reach, offset, 1.0 / math.sqrt(all_points)),
        (
            shape((plane_points, PAIR)), shape((reach, 2 * points, PAIR)), shape((reach, 2 * points, PAIR)),
            shape((group, 2 * points, PAIR), f32), shape((PAIR, width), f32),
        ),
        flops=16 * work, moved=40 * plane_points * PAIR,
        grid_spec=pltpu.PrefetchScalarGridSpec(
            num_scalar_prefetch=1,
            grid=(blocks,),
            in_specs=[
                start_spec, chance_spec, column_spec, inverse_spec, whole((plane_points, PAIR)),
                whole((total, PAIR)), whole((total, PAIR)), whole((PAIR, total)), whole((PAIR, width)),
            ] + [whole((points, width))] * group,
            out_specs=(
                row_spec, whole((reach, 2 * points, PAIR)), whole((reach, 2 * points, PAIR)),
                whole((group, 2 * points, PAIR)), whole((PAIR, width)),
            ),
            scratch_shapes=[
                pltpu.VMEM((plane_points, width), bf16), pltpu.VMEM((total, PAIR), f32),
                pltpu.VMEM((total, PAIR), f32), pltpu.VMEM((2, HEAD, QBLOCK), f32),
            ],
        ),
    )(place_list, starts, chances, mixed_t, inverse, q_all, k_all, v_all, kt_all, own_weight, *cots)

    from_above = permute(low_part, lambda i: i - group)
    from_below = permute(high_part, lambda i: i + group)
    shares = []
    for s in range(planes):
        piece = lax.dynamic_slice_in_dim(weight_part, (plane + s) % planes * part_rows, part_rows, 0)
        shares.append(permute(piece, lambda i, s=s: i % group * planes + (i // group + s) % planes))
    first = jnp.concatenate(
        [mixed.reshape(group, points, PAIR), grad_q.reshape(group, points, PAIR)], axis=1
    )
    first = lax.all_to_all(first, "seq", 0, 0, tiled=True, axis_index_groups=groups)
    layer_out, grad_queries = call(
        functools.partial(layer_kernel, points), (shape((points, width)), shape((points, width))),
        flops=2 * points * width * width, moved=2 * width * width + 8 * points * width,
        grid_spec=pltpu.PrefetchScalarGridSpec(
            num_scalar_prefetch=1,
            grid=(1,),
            in_specs=[whole(first.shape)] + [whole((PAIR, width))] * group,
            out_specs=(whole((points, width)), whole((points, width))),
        ),
    )(place_list, first, *weights)
    summed = call(
        add_kernel, shape((group, 2 * points, PAIR)), moved=16 * points * width,
    )(own_part, from_below, from_above)
    summed = lax.all_to_all(summed, "seq", 0, 0, tiled=True, axis_index_groups=groups)
    grad_keys, grad_values = call(
        functools.partial(split_kernel, points), (shape((points, width)), shape((points, width))),
        moved=8 * points * width,
    )(summed)
    grad_weight = sum(shares[1:], shares[0]).reshape(part_rows * width)
    return (layer_out, grad_queries, grad_keys, grad_values, grad_weight)


def solution(mesh):
    rows = P("seq", None)
    return jax.shard_map(
        per_device,
        mesh=mesh,
        in_specs=(rows, rows, rows, P("seq"), rows, P(), P("seq")),
        out_specs=(rows, rows, rows, rows, P("seq")),
        check_vma=False,
    )
```

time: 740 us -> 205 us (0.28)
  local copies, waits for them, and re-layouts: 215 us -> 7.81 us
  waiting for transfers between devices: 165 us -> 47.5 us
  starting transfers between devices: 167 us -> 61.5 us
  matrix products: 104 us -> 0 us
  Pallas kernels: 0 us -> 79.6 us
  other arithmetic: 39.8 us -> 4.27 us
  loops' own time: 26.8 us -> 0 us
  between operations: 14.9 us -> 1.08 us
    ppermute x42 -> x26, waiting for transfers between devices: 165 us -> 32.2 us  [permute(): lax.ppermute(block, 'seq', [(i, move(i)) for i in devices if move(i) in d...]
    ppermute x42 -> x26, starting transfers between devices: 167 us -> 49 us  [permute(): lax.ppermute(block, 'seq', [(i, move(i)) for i in devices if move(i) in d...]
    dynamic_slice x120 -> x2, local copies, waits for them, and re-layouts: 117 us -> 0.78 us  [the longest x1 0.74 us: per_device(): lax.dynamic_slice_in_dim(order, planes - 1 - plane, planes, 0)]
    dot_general x59 -> x0, matrix products: 104 us -> none  [the longest x8 18.9 us: query_group(): jnp.einsum('hqk,khd->qhd', slopes, key_part, preferred_element_type=jnp.f...]
    pallas_call x0 -> x6, Pallas kernels: none -> 79.6 us  [the longest x1 41.3 us: per_device(): call(functools.partial(backward_kernel, points, reach, offset, 1.0 / math...]
    unnamed x70 -> x49, local copies, waits for them, and re-layouts: 51.2 us -> 5.77 us
    another operation x3 -> x0, loops' own time: 26.8 us -> none  [the longest x1 10.9 us: per_device(): key_groups, value_groups = lax.map(key_group, group_list)]
    concatenate x14 -> x1, other arithmetic: 22.8 us -> 1.92 us  [per_device(): jnp.concatenate([mixed.reshape(group, points, PAIR), grad_q.reshape(group...]
  transfers between devices with their start and end apart: 44 -> 29, of which waited for: 14 -> 9; matrix products, arithmetic and copies ran while one was open for 30% -> 3% of each run, Pallas kernels for 0% -> 18%
where the time goes in v1:
time: 205 us; the launch traced here: 202 us
  Pallas kernels  79.6 us (39%)
  starting transfers between devices  61.5 us (30%)
  waiting for transfers between devices  47.5 us (23%)
  local copies, waits for them, and re-layouts  7.81 us (4%)
  other arithmetic  4.27 us (2%)
    ppermute x26, starting transfers between devices, permute(): lax.ppermute(block, 'seq', [(i, move(i)) for i in devices if move(i) in d...  49 us
    pallas_call x1, Pallas kernels, per_device(): call(functools.partial(backward_kernel, points, reach, offset, 1.0 / math...  41.3 us
    ppermute x26, waiting for transfers between devices, permute(): lax.ppermute(block, 'seq', [(i, move(i)) for i in devices if move(i) in d...  32.2 us
    pallas_call x1, Pallas kernels, per_device(): call(functools.partial(forward_kernel, points, reach, offset), (shape((bl...  27.8 us
    all_to_all x1, waiting for transfers between devices, per_device(): lax.all_to_all(packed, 'seq', 0, 0, tiled=True, axis_index_groups=groups)  10.7 us
    unnamed x49, local copies, waits for them, and re-layouts  5.77 us
    all_to_all x1, starting transfers between devices, per_device(): lax.all_to_all(first, 'seq', 0, 0, tiled=True, axis_index_groups=groups)  5.27 us
    all_to_all x1, waiting for transfers between devices, per_device(): lax.all_to_all(first, 'seq', 0, 0, tiled=True, axis_index_groups=groups)  4.53 us
  transfers between devices with their start and end apart: 29, of which 9 were waited for; matrix products, arithmetic and copies ran while one was open for 3% of the time, Pallas kernels for 18%

profile of v1, /device:TPU:8, one launch (start us, length us, event | category | flops | bytes accessed | tf_op | source)
XLA Modules:
  0.0 201.8 jit_solution(5095409707764037654)
XLA Ops:
  0.6 0.9 reshape.96
  1.5 5.4 %collective-permute-start.2 = (bf16[32,1024]{1,0:T(8,128)(2,1)S(1)}, bf16[32,1024]{1,0:T(8,128)(2,1)S(1)}, u32[]{:S(2)}, u32[]{:S(2)}) collective-permute-start(bf16[32,1024]{1,0:T(8,128)(2,1)S(1)} %reshape.96), channel_id=1, source_target_pairs={{0,24},{1,0},{2,8},{3,16},{4,25},{5,1},{6,9},{7,17},{8,26},{9,2},{... | collective-permute-start | bytes 196616 | tf_op jit(solution)/shard_map/ppermute | solution.py:253
  6.9 0.4 collective-permute-start.3
  7.4 1.9 collective-permute-start.4
  9.3 5.4 %collective-permute-start.5 = (bf16[32,1024]{1,0:T(8,128)(2,1)S(1)}, bf16[32,1024]{1,0:T(8,128)(2,1)S(1)}, u32[]{:S(2)}, u32[]{:S(2)}) collective-permute-start(bf16[32,1024]{1,0:T(8,128)(2,1)S(1)} %reshape.96), channel_id=1, source_target_pairs={{0,0},{1,8},{2,16},{3,24},{4,1},{5,9},{6,17},{7,25},{8,2},{9,10},{... | collective-permute-start | bytes 196616 | tf_op jit(solution)/shard_map/ppermute | solution.py:253
  14.7 0.7 fusion.5
  15.4 0.7 fusion.3.extra_ref
  16.1 2.3 %shard_map.110 = bf16[8,496,128]{2,1,0:T(8,128)(2,1)} custom-call(bf16[160,1024]{1,0:T(8,128)(2,1)} %q_ref.1, bf16[160,1024]{1,0:T(8,128)(2,1)} %k_ref.1, bf16[160,1024]{1,0:T(8,128)(2,1)} %v_ref.1, bf16[16,128]{1,0:T(8,128)(2,1)} %fusion.3.extra_ref), custom_call_target="tpu_custom_call" | custom-call | bytes 1966080 | tf_op jit(solution)/shard_map/pallas_call | solution.py:290
  18.4 3.7 %all-to-all-start = ((bf16[8,496,128]{2,1,0:T(8,128)(2,1)}), bf16[8,496,128]{2,1,0:T(8,128)(2,1)S(1)}, u32[]{:S(2)}, u32[]{:S(2)}) async-start(bf16[8,496,128]{2,1,0:T(8,128)(2,1)} %shard_map.110), calls=%async_computation | async-start | bytes 2031616 | tf_op jit(solution)/shard_map/all_to_all | solution.py:304
  22.1 1.9 collective-permute-start.9
  24.1 0.1 copy.14
  24.2 0.1 reduce
  24.4 0.1 select_reduce_fusion
  24.5 1.5 collective-permute-start.11
  26.0 0.2 collective-permute-start.7
  26.3 0.7 constant_dynamic-slice_fusion.4
  27.1 10.7 %all-to-all-done.x_ref = bf16[8,496,128]{2,1,0:T(8,128)(2,1)S(1)} async-done(((bf16[8,496,128]{2,1,0:T(8,128)(2,1)}), bf16[8,496,128]{2,1,0:T(8,128)(2,1)S(1)}, u32[]{:S(2)}, u32[]{:S(2)}) %all-to-all-start) | async-done | bytes 1015840 | tf_op jit(solution)/shard_map/all_to_all | solution.py:304
  37.8 0.2 fusion.6
  38.0 3.4 %collective-permute-start = (bf16[7,320,128]{2,1,0:T(8,128)(2,1)S(1)}, bf16[7,320,128]{2,1,0:T(8,128)(2,1)S(1)}, u32[]{:S(2)}, u32[]{:S(2)}) collective-permute-start(bf16[7,320,128]{2,1,0:T(8,128)(2,1)S(1)} %get-tuple-element.40), channel_id=1, source_target_pairs={{0,8},{1,9},{2,10},{3,11},{4,12},{5,13},{6,14},{7,15},{8,16},{9,17... | collective-permute-start | bytes 1720328 | tf_op jit(solution)/shard_map/ppermute | solution.py:253
  41.4 2.5 %collective-permute-start.1 = (bf16[7,320,128]{2,1,0:T(8,128)(2,1)S(1)}, bf16[7,320,128]{2,1,0:T(8,128)(2,1)S(1)}, u32[]{:S(2)}, u32[]{:S(2)}) collective-permute-start(bf16[7,320,128]{2,1,0:T(8,128)(2,1)S(1)} %get-tuple-element.39), channel_id=1, source_target_pairs={{8,0},{9,1},{10,2},{11,3},{12,4},{13,5},{14,6},{15,7},{16,8},{17,9... | collective-permute-start | bytes 1720328 | tf_op jit(solution)/shard_map/ppermute | solution.py:253
  43.9 0.1 slice_add_fusion
  44.0 0.1 reshape.94
  44.1 0.6 subtract_add_fusion.start_ref
  44.7 5.6 %collective-permute-done.9.rest_4_ = bf16[160,1024]{1,0:T(8,128)(2,1)} collective-permute-done((bf16[160,1024]{1,0:T(8,128)(2,1)}, bf16[160,1024]{1,0:T(8,128)(2,1)}, u32[]{:S(2)}, u32[]{:S(2)}) %collective-permute-start.9) | collective-permute-done | bytes 327712 | tf_op jit(solution)/shard_map/ppermute | solution.py:253
  50.3 0.5 collective-permute-start.10
  50.8 0.1 collective-permute-start.12
  50.9 0.2 collective-permute-done.low_ref
  51.1 0.2 collective-permute-start.8
  51.3 3.2 %collective-permute-done.1.high_ref = bf16[7,320,128]{2,1,0:T(8,128)(2,1)S(1)} collective-permute-done((bf16[7,320,128]{2,1,0:T(8,128)(2,1)S(1)}, bf16[7,320,128]{2,1,0:T(8,128)(2,1)S(1)}, u32[]{:S(2)}, u32[]{:S(2)}) %collective-permute-start.1) | collective-permute-done | bytes 573472 | tf_op jit(solution)/shard_map/ppermute | solution.py:253
  54.6 0.8 copy-done.17
  55.4 27.8 %shard_map.111 = (bf16[5,2,2560,256]{3,2,1,0:T(8,128)(2,1)}, bf16[128,1280]{1,0:T(8,128)(2,1)}, bf16[1280,128]{1,0:T(8,128)(2,1)}, f32[8,1280]{1,0:T(8,128)}, bf...) custom-call(bf16[8,496,128]{2,1,0:T(8,128)(2,1)} %copy-done, ...), custom_call_target="tpu_custom_call" | custom-call | flops 6710886400 | bytes 6553600 | tf_op jit(solution)/shard_map/pallas_call | solution.py:322
  83.3 0.7 copy-done.18
  83.9 0.1 copy-done.19
  84.1 41.3 %shard_map.112 = (bf16[1280,128]{1,0:T(8,128)(2,1)}, bf16[7,320,128]{2,1,0:T(8,128)(2,1)}, bf16[7,320,128]{2,1,0:T(8,128)(2,1)}, f32[8,320,128]{2,1,0:T(8,128)}, f32[128,1024]{1,0:T(8,128)}) custom-call(s32[1]{0:T(128)} %bitcast.place_ref, s32[1,1280]{1,0:T(1,128)} %subtract_add_fusion.start_ref, bf16[5,2,2560,256]{3,2,1,0:T(8,128)(2,1)} %get-tuple-element.23.p_ref, ...), custom_call_target="tpu_custom_call" | custom-call | flops 13421772800 | bytes 6553600 | tf_op jit(solution)/shard_map/pallas_call | solution.py:343
  125.4 1.9 collective-permute-start.20
  127.3 4.0 %collective-permute-start.21 = (bf16[7,320,128]{2,1,0:T(8,128)(2,1)}, bf16[7,320,128]{2,1,0:T(8,128)(2,1)S(1)}, u32[]{:S(2)}, u32[]{:S(2)}) collective-permute-start(bf16[7,320,128]{2,1,0:T(8,128)(2,1)} %get-tuple-element.35), channel_id=1, source_target_pairs={{8,0},{9,1},{10,2},{11,3},{12,4},{13,5},{14,6},{15,7},{16,8},{17,9... | collective-permute-start | bytes 1720328 | tf_op jit(solution)/shard_map/ppermute | solution.py:253
  131.3 1.9 pad_maximum_fusion
  133.2 5.3 %all-to-all-start.1 = ((bf16[8,320,128]{2,1,0:T(8,128)(2,1)}), bf16[8,320,128]{2,1,0:T(8,128)(2,1)S(1)}, u32[]{:S(2)}, u32[]{:S(2)}) async-start(bf16[8,320,128]{2,1,0:T(8,128)(2,1)} %pad_maximum_fusion), calls=%async_computation.1 | async-start | bytes 1310720 | tf_op jit(solution)/shard_map/all_to_all | solution.py:377
  138.5 2.3 %collective-permute-start.14 = (bf16[128,1024]{1,0:T(8,128)(2,1)S(1)}, bf16[128,1024]{1,0:T(8,128)(2,1)S(1)}, u32[]{:S(2)}, u32[]{:S(2)}) collective-permute-start(bf16[128,1024]{1,0:T(8,128)(2,1)S(1)} %bitcast.29), channel_id=1, source_target_pairs={{0,2},{1,3},{2,0},{3,1},{4,6},{5,7},{6,4},{7,5},{8,10},{9,11},{10,... | collective-permute-start | bytes 786440 | tf_op jit(solution)/shard_map/ppermute | solution.py:253
  140.8 1.2 collective-permute-start.16
  142.0 0.8 copy-done.4
  142.8 0.2 copy-done.5
  143.0 2.7 %shard_map.114 = bf16[8,320,128]{2,1,0:T(8,128)(2,1)} custom-call(f32[8,320,128]{2,1,0:T(8,128)} %get-tuple-element.33.own_ref, bf16[7,320,128]{2,1,0:T(8,128)(2,1)} %copy-done.4, bf16[7,320,128]{2,1,0:T(8,128)(2,1)} %copy-done.5), custom_call_target="tpu_custom_call" | custom-call | bytes 2621440 | tf_op jit(solution)/shard_map/pallas_call | solution.py:388
  145.7 4.5 %all-to-all-done.1.y_ref = bf16[8,320,128]{2,1,0:T(8,128)(2,1)S(1)} async-done(((bf16[8,320,128]{2,1,0:T(8,128)(2,1)}), bf16[8,320,128]{2,1,0:T(8,128)(2,1)S(1)}, u32[]{:S(2)}, u32[]{:S(2)}) %all-to-all-start.1) | async-done | bytes 655392 | tf_op jit(solution)/shard_map/all_to_all | solution.py:377
  150.2 3.5 %all-to-all-start.2 = ((bf16[8,320,128]{2,1,0:T(8,128)(2,1)}), bf16[8,320,128]{2,1,0:T(8,128)(2,1)S(1)}, u32[]{:S(2)}, u32[]{:S(2)}) async-start(bf16[8,320,128]{2,1,0:T(8,128)(2,1)} %shard_map.114), calls=%async_computation.2 | async-start | bytes 1310720 | tf_op jit(solution)/shard_map/all_to_all | solution.py:391
  153.8 2.9 %collective-permute-start.18 = (bf16[128,1024]{1,0:T(8,128)(2,1)S(1)}, bf16[128,1024]{1,0:T(8,128)(2,1)S(1)}, u32[]{:S(2)}, u32[]{:S(2)}) collective-permute-start(bf16[128,1024]{1,0:T(8,128)(2,1)S(1)} %bitcast.31), channel_id=1, source_target_pairs={{0,6},{1,7},{2,4},{3,5},{4,2},{5,3},{6,0},{7,1},{8,14},{9,15},{10,... | collective-permute-start | bytes 786440 | tf_op jit(solution)/shard_map/ppermute | solution.py:253
  156.7 1.9 collective-permute-start.22
  158.6 4.8 %collective-permute-start.23 = (f32[32,1024]{1,0:T(8,128)S(1)}, f32[32,1024]{1,0:T(8,128)S(1)}, u32[]{:S(2)}, u32[]{:S(2)}) collective-permute-start(f32[32,1024]{1,0:T(8,128)S(1)} %get-tuple-element.41), channel_id=1, source_target_pairs={{0,1},{1,5},{2,9},{3,13},{4,17},{5,21},{6,25},{7,29},{8,2},{9,6},{... | collective-permute-start | bytes 393224 | tf_op jit(solution)/shard_map/ppermute | solution.py:253
  163.4 0.0 copy-start.8
  163.4 0.1 collective-permute-start.24
  163.5 2.4 %collective-permute-start.25 = (f32[32,1024]{1,0:T(8,128)S(1)}, f32[32,1024]{1,0:T(8,128)S(1)}, u32[]{:S(2)}, u32[]{:S(2)}) collective-permute-start(f32[32,1024]{1,0:T(8,128)S(1)} %get-tuple-element.42), channel_id=1, source_target_pairs={{0,3},{1,7},{2,11},{3,15},{4,19},{5,23},{6,27},{7,31},{8,0},{9,4},... | collective-permute-start | bytes 393224 | tf_op jit(solution)/shard_map/ppermute | solution.py:253
  166.0 4.4 %collective-permute-done.18.rest_6_ = bf16[128,1024]{1,0:T(8,128)(2,1)S(1)} collective-permute-done((bf16[128,1024]{1,0:T(8,128)(2,1)S(1)}, bf16[128,1024]{1,0:T(8,128)(2,1)S(1)}, u32[]{:S(2)}, u32[]{:S(2)}) %collective-permute-start.18) | collective-permute-done | bytes 262176 | tf_op jit(solution)/shard_map/ppermute | solution.py:253
  170.4 15.1 %collective-permute-done.22 = f32[32,1024]{1,0:T(8,128)S(1)} collective-permute-done((f32[32,1024]{1,0:T(8,128)S(1)}, f32[32,1024]{1,0:T(8,128)S(1)}, u32[]{:S(2)}, u32[]{:S(2)}) %collective-permute-start.22) | collective-permute-done | bytes 131104 | tf_op jit(solution)/shard_map/ppermute | solution.py:253
  185.5 4.0 %collective-permute-start.15 = (bf16[128,1024]{1,0:T(8,128)(2,1)S(1)}, bf16[128,1024]{1,0:T(8,128)(2,1)S(1)}, u32[]{:S(2)}, u32[]{:S(2)}) collective-permute-start(bf16[128,1024]{1,0:T(8,128)(2,1)S(1)} %collective-permute-done.14.rest_2_), channel_id=1, source_target_pairs={{0,1},{1,0},{2,3},{3,2},{4,5},{5,4},{6,7},{7,6},{8,9},{9,8},{10,11... | collective-permute-start | bytes 786440 | tf_op jit(solution)/shard_map/ppermute | solution.py:253
  189.6 1.6 collective-permute-done.24
  191.1 2.0 collective-permute-done.25
  193.2 0.7 copy.16
  193.9 0.6 copy-done.11
  194.6 0.1 copy-done.12
  194.7 0.1 copy-done.13
  194.8 0.7 copy-done.14
  195.4 3.4 %shard_map.113 = (bf16[160,1024]{1,0:T(8,128)(2,1)}, bf16[160,1024]{1,0:T(8,128)(2,1)}) custom-call(s32[1]{0:T(128)} %bitcast.place_ref, bf16[8,320,128]{2,1,0:T(8,128)(2,1)} %copy-done.2, bf16[128,1024]{1,0:T(8,128)(2,1)} %bitcast.28, bf16[128,1024]{1,0:T(8,128)(2,1)} %copy-done.11, bf16[128,1024]{1,0:T(8,128)(2,1)} %copy-done.8, ...), custom_call_target="tpu_custom_call" | custom-call | flops 335544320 | bytes 3407872 | tf_op jit(solution)/shard_map/pallas_call | solution.py:378
  198.8 0.9 copy-done.1
  199.7 2.1 %shard_map.115 = (bf16[160,1024]{1,0:T(8,128)(2,1)}, bf16[160,1024]{1,0:T(8,128)(2,1)}) custom-call(bf16[8,320,128]{2,1,0:T(8,128)(2,1)} %copy-done.1), custom_call_target="tpu_custom_call" | custom-call | bytes 1310720 | tf_op jit(solution)/shard_map/pallas_call | solution.py:392
  (67 shorter events, 0.3 us)
Async XLA Ops:
  1.5 23.0 %collective-permute-start.2 = (bf16[32,1024]{1,0:T(8,128)(2,1)S(1)}, bf16[32,1024]{1,0:T(8,128)(2,1)S(1)}, u32[]{:S(2)}, u32[]{:S(2)}) collective-permute-start(bf16[32,1024]{1,0:T(8,128)(2,1)S(1)} %reshape.96), channel_id=1, source_target_pairs={{0,24},{1,0},{2,8},{3,16},{4,25},{5,1},{6,9},{7,17},{8,26},{9,2},{... | collective-permute-start | bytes 196616 | tf_op jit(solution)/shard_map/ppermute | solution.py:253
  6.9 19.1 %collective-permute-start.3 = (bf16[32,1024]{1,0:T(8,128)(2,1)S(1)}, bf16[32,1024]{1,0:T(8,128)(2,1)S(1)}, u32[]{:S(2)}, u32[]{:S(2)}) collective-permute-start(bf16[32,1024]{1,0:T(8,128)(2,1)S(1)} %reshape.96), channel_id=1, source_target_pairs={{0,16},{1,24},{2,0},{3,8},{4,17},{5,25},{6,1},{7,9},{8,18},{9,26},... | collective-permute-start | bytes 196616 | tf_op jit(solution)/shard_map/ppermute | solution.py:253
  7.4 18.9 %collective-permute-start.4 = (bf16[32,1024]{1,0:T(8,128)(2,1)S(1)}, bf16[32,1024]{1,0:T(8,128)(2,1)S(1)}, u32[]{:S(2)}, u32[]{:S(2)}) collective-permute-start(bf16[32,1024]{1,0:T(8,128)(2,1)S(1)} %reshape.96), channel_id=1, source_target_pairs={{0,8},{1,16},{2,24},{3,0},{4,9},{5,17},{6,25},{7,1},{8,10},{9,18},... | collective-permute-start | bytes 196616 | tf_op jit(solution)/shard_map/ppermute | solution.py:253
  9.3 17.0 %collective-permute-start.5 = (bf16[32,1024]{1,0:T(8,128)(2,1)S(1)}, bf16[32,1024]{1,0:T(8,128)(2,1)S(1)}, u32[]{:S(2)}, u32[]{:S(2)}) collective-permute-start(bf16[32,1024]{1,0:T(8,128)(2,1)S(1)} %reshape.96), channel_id=1, source_target_pairs={{0,0},{1,8},{2,16},{3,24},{4,1},{5,9},{6,17},{7,25},{8,2},{9,10},{... | collective-permute-start | bytes 196616 | tf_op jit(solution)/shard_map/ppermute | solution.py:253
  18.4 5.6 %copy-start.15 = (s32[25]{0:T(128)S(1)}, s32[25]{0:T(128)}, u32[]{:S(2)}) copy-start(s32[25]{0:T(128)} %param.12) | copy-start | bytes 304
  18.4 19.3 %all-to-all-start = ((bf16[8,496,128]{2,1,0:T(8,128)(2,1)}), bf16[8,496,128]{2,1,0:T(8,128)(2,1)S(1)}, u32[]{:S(2)}, u32[]{:S(2)}) async-start(bf16[8,496,128]{2,1,0:T(8,128)(2,1)} %shard_map.110), calls=%async_computation | async-start | bytes 2031616 | tf_op jit(solution)/shard_map/all_to_all | solution.py:304
  22.1 28.2 %collective-permute-start.9 = (bf16[160,1024]{1,0:T(8,128)(2,1)}, bf16[160,1024]{1,0:T(8,128)(2,1)}, u32[]{:S(2)}, u32[]{:S(2)}) collective-permute-start(bf16[160,1024]{1,0:T(8,128)(2,1)} %rest_0_.1), channel_id=1, source_target_pairs={{0,4},{1,5},{2,6},{3,7},{4,0},{5,1},{6,2},{7,3},{8,12},{9,13},{10,... | collective-permute-start | bytes 983048 | tf_op jit(solution)/shard_map/ppermute | solution.py:253
  24.5 25.8 %collective-permute-start.11 = (bf16[160,1024]{1,0:T(8,128)(2,1)}, bf16[160,1024]{1,0:T(8,128)(2,1)}, u32[]{:S(2)}, u32[]{:S(2)}) collective-permute-start(bf16[160,1024]{1,0:T(8,128)(2,1)} %rest_0_.1), channel_id=1, source_target_pairs={{0,6},{1,7},{2,4},{3,5},{4,2},{5,3},{6,0},{7,1},{8,14},{9,15},{10,... | collective-permute-start | bytes 983048 | tf_op jit(solution)/shard_map/ppermute | solution.py:253
  26.0 24.8 %collective-permute-start.7 = (bf16[160,1024]{1,0:T(8,128)(2,1)}, bf16[160,1024]{1,0:T(8,128)(2,1)}, u32[]{:S(2)}, u32[]{:S(2)}) collective-permute-start(bf16[160,1024]{1,0:T(8,128)(2,1)} %rest_0_.1), channel_id=1, source_target_pairs={{0,2},{1,3},{2,0},{3,1},{4,6},{5,7},{6,4},{7,5},{8,10},{9,11},{10,... | collective-permute-start | bytes 983048 | tf_op jit(solution)/shard_map/ppermute | solution.py:253
  37.8 16.8 %copy-start = (bf16[8,496,128]{2,1,0:T(8,128)(2,1)}, bf16[8,496,128]{2,1,0:T(8,128)(2,1)S(1)}, u32[]{:S(2)}) copy-start(bf16[8,496,128]{2,1,0:T(8,128)(2,1)S(1)} %all-to-all-done.x_ref) | copy-start | bytes 3047428
  38.0 13.1 %collective-permute-start = (bf16[7,320,128]{2,1,0:T(8,128)(2,1)S(1)}, bf16[7,320,128]{2,1,0:T(8,128)(2,1)S(1)}, u32[]{:S(2)}, u32[]{:S(2)}) collective-permute-start(bf16[7,320,128]{2,1,0:T(8,128)(2,1)S(1)} %get-tuple-element.40), channel_id=1, source_target_pairs={{0,8},{1,9},{2,10},{3,11},{4,12},{5,13},{6,14},{7,15},{8,16},{9,17... | collective-permute-start | bytes 1720328 | tf_op jit(solution)/shard_map/ppermute | solution.py:253
  41.4 13.1 %collective-permute-start.1 = (bf16[7,320,128]{2,1,0:T(8,128)(2,1)S(1)}, bf16[7,320,128]{2,1,0:T(8,128)(2,1)S(1)}, u32[]{:S(2)}, u32[]{:S(2)}) collective-permute-start(bf16[7,320,128]{2,1,0:T(8,128)(2,1)S(1)} %get-tuple-element.39), channel_id=1, source_target_pairs={{8,0},{9,1},{10,2},{11,3},{12,4},{13,5},{14,6},{15,7},{16,8},{17,9... | collective-permute-start | bytes 1720328 | tf_op jit(solution)/shard_map/ppermute | solution.py:253
  50.3 32.9 %collective-permute-start.6 = (bf16[160,1024]{1,0:T(8,128)(2,1)}, bf16[160,1024]{1,0:T(8,128)(2,1)S(1)}, u32[]{:S(2)}, u32[]{:S(2)}) collective-permute-start(bf16[160,1024]{1,0:T(8,128)(2,1)} %rest_0_.1), channel_id=1, source_target_pairs={{0,1},{1,0},{2,3},{3,2},{4,5},{5,4},{6,7},{7,6},{8,9},{9,8},{10,11... | collective-permute-start | bytes 983048 | tf_op jit(solution)/shard_map/ppermute | solution.py:253
  50.3 32.9 %collective-permute-start.10 = (bf16[160,1024]{1,0:T(8,128)(2,1)}, bf16[160,1024]{1,0:T(8,128)(2,1)}, u32[]{:S(2)}, u32[]{:S(2)}) collective-permute-start(bf16[160,1024]{1,0:T(8,128)(2,1)} %collective-permute-done.9.rest_4_), channel_id=1, source_target_pairs={{0,1},{1,0},{2,3},{3,2},{4,5},{5,4},{6,7},{7,6},{8,9},{9,8},{10,11... | collective-permute-start | bytes 983048 | tf_op jit(solution)/shard_map/ppermute | solution.py:253
  50.8 32.4 %collective-permute-start.12 = (bf16[160,1024]{1,0:T(8,128)(2,1)}, bf16[160,1024]{1,0:T(8,128)(2,1)}, u32[]{:S(2)}, u32[]{:S(2)}) collective-permute-start(bf16[160,1024]{1,0:T(8,128)(2,1)} %collective-permute-done.11.rest_6_), channel_id=1, source_target_pairs={{0,1},{1,0},{2,3},{3,2},{4,5},{5,4},{6,7},{7,6},{8,9},{9,8},{10,11... | collective-permute-start | bytes 983048 | tf_op jit(solution)/shard_map/ppermute | solution.py:253
  51.1 3.4 %copy-start.16 = (bf16[7,320,128]{2,1,0:T(8,128)(2,1)}, bf16[7,320,128]{2,1,0:T(8,128)(2,1)S(1)}, u32[]{:S(2)}) copy-start(bf16[7,320,128]{2,1,0:T(8,128)(2,1)S(1)} %collective-permute-done.low_ref) | copy-start | bytes 1720324
  51.1 32.1 %collective-permute-start.8 = (bf16[160,1024]{1,0:T(8,128)(2,1)}, bf16[160,1024]{1,0:T(8,128)(2,1)S(1)}, u32[]{:S(2)}, u32[]{:S(2)}) collective-permute-start(bf16[160,1024]{1,0:T(8,128)(2,1)} %collective-permute-done.7.rest_2_), channel_id=1, source_target_pairs={{0,1},{1,0},{2,3},{3,2},{4,5},{5,4},{6,7},{7,6},{8,9},{9,8},{10,11... | collective-permute-start | bytes 983048 | tf_op jit(solution)/shard_map/ppermute | solution.py:253
  54.6 0.8 copy-start.17
  83.2 0.7 copy-start.18
  83.3 0.8 copy-start.19
  84.1 47.2 %copy-start.7 = (bf16[1280,128]{1,0:T(8,128)(2,1)S(1)}, bf16[1280,128]{1,0:T(8,128)(2,1)}, u32[]{:S(2)}) copy-start(bf16[1280,128]{1,0:T(8,128)(2,1)} %get-tuple-element.22) | copy-start | bytes 983044
  125.4 16.6 %collective-permute-start.20 = (bf16[7,320,128]{2,1,0:T(8,128)(2,1)}, bf16[7,320,128]{2,1,0:T(8,128)(2,1)S(1)}, u32[]{:S(2)}, u32[]{:S(2)}) collective-permute-start(bf16[7,320,128]{2,1,0:T(8,128)(2,1)} %get-tuple-element.34), channel_id=1, source_target_pairs={{0,8},{1,9},{2,10},{3,11},{4,12},{5,13},{6,14},{7,15},{8,16},{9,17... | collective-permute-start | bytes 1720328 | tf_op jit(solution)/shard_map/ppermute | solution.py:253
  127.3 14.7 %collective-permute-start.21 = (bf16[7,320,128]{2,1,0:T(8,128)(2,1)}, bf16[7,320,128]{2,1,0:T(8,128)(2,1)S(1)}, u32[]{:S(2)}, u32[]{:S(2)}) collective-permute-start(bf16[7,320,128]{2,1,0:T(8,128)(2,1)} %get-tuple-element.35), channel_id=1, source_target_pairs={{8,0},{9,1},{10,2},{11,3},{12,4},{13,5},{14,6},{15,7},{16,8},{17,9... | collective-permute-start | bytes 1720328 | tf_op jit(solution)/shard_map/ppermute | solution.py:253
  131.3 7.2 %copy-start.3 = (bf16[4,32,1024]{2,1,0:T(8,128)(2,1)S(1)}, bf16[4,32,1024]{2,1,0:T(8,128)(2,1)}, u32[]{:S(2)}) copy-start(bf16[4,32,1024]{2,1,0:T(8,128)(2,1)} %constant_dynamic-slice_fusion.4) | copy-start | bytes 786436
  133.2 17.0 %all-to-all-start.1 = ((bf16[8,320,128]{2,1,0:T(8,128)(2,1)}), bf16[8,320,128]{2,1,0:T(8,128)(2,1)S(1)}, u32[]{:S(2)}, u32[]{:S(2)}) async-start(bf16[8,320,128]{2,1,0:T(8,128)(2,1)} %pad_maximum_fusion), calls=%async_computation.1 | async-start | bytes 1310720 | tf_op jit(solution)/shard_map/all_to_all | solution.py:377
  138.5 24.9 %collective-permute-start.14 = (bf16[128,1024]{1,0:T(8,128)(2,1)S(1)}, bf16[128,1024]{1,0:T(8,128)(2,1)S(1)}, u32[]{:S(2)}, u32[]{:S(2)}) collective-permute-start(bf16[128,1024]{1,0:T(8,128)(2,1)S(1)} %bitcast.29), channel_id=1, source_target_pairs={{0,2},{1,3},{2,0},{3,1},{4,6},{5,7},{6,4},{7,5},{8,10},{9,11},{10,... | collective-permute-start | bytes 786440 | tf_op jit(solution)/shard_map/ppermute | solution.py:253
  140.8 22.7 %collective-permute-start.16 = (bf16[128,1024]{1,0:T(8,128)(2,1)S(1)}, bf16[128,1024]{1,0:T(8,128)(2,1)S(1)}, u32[]{:S(2)}, u32[]{:S(2)}) collective-permute-start(bf16[128,1024]{1,0:T(8,128)(2,1)S(1)} %bitcast.30), channel_id=1, source_target_pairs={{0,4},{1,5},{2,6},{3,7},{4,0},{5,1},{6,2},{7,3},{8,12},{9,13},{10,... | collective-permute-start | bytes 786440 | tf_op jit(solution)/shard_map/ppermute | solution.py:253
  142.0 0.8 copy-start.4
  142.0 1.0 copy-start.5
  145.7 10.9 %copy-start.6 = (f32[128,1024]{1,0:T(8,128)S(1)}, f32[128,1024]{1,0:T(8,128)}, u32[]{:S(2)}) copy-start(f32[128,1024]{1,0:T(8,128)} %get-tuple-element.38) | copy-start | bytes 1572868
  150.2 43.0 %copy-start.2 = (bf16[8,320,128]{2,1,0:T(8,128)(2,1)}, bf16[8,320,128]{2,1,0:T(8,128)(2,1)S(1)}, u32[]{:S(2)}) copy-start(bf16[8,320,128]{2,1,0:T(8,128)(2,1)S(1)} %all-to-all-done.1.y_ref) | copy-start | bytes 1966084
  150.2 48.6 %all-to-all-start.2 = ((bf16[8,320,128]{2,1,0:T(8,128)(2,1)}), bf16[8,320,128]{2,1,0:T(8,128)(2,1)S(1)}, u32[]{:S(2)}, u32[]{:S(2)}) async-start(bf16[8,320,128]{2,1,0:T(8,128)(2,1)} %shard_map.114), calls=%async_computation.2 | async-start | bytes 1310720 | tf_op jit(solution)/shard_map/all_to_all | solution.py:391
  153.8 16.7 %collective-permute-start.18 = (bf16[128,1024]{1,0:T(8,128)(2,1)S(1)}, bf16[128,1024]{1,0:T(8,128)(2,1)S(1)}, u32[]{:S(2)}, u32[]{:S(2)}) collective-permute-start(bf16[128,1024]{1,0:T(8,128)(2,1)S(1)} %bitcast.31), channel_id=1, source_target_pairs={{0,6},{1,7},{2,4},{3,5},{4,2},{5,3},{6,0},{7,1},{8,14},{9,15},{10,... | collective-permute-start | bytes 786440 | tf_op jit(solution)/shard_map/ppermute | solution.py:253
  156.7 28.9 %collective-permute-start.22 = (f32[32,1024]{1,0:T(8,128)S(1)}, f32[32,1024]{1,0:T(8,128)S(1)}, u32[]{:S(2)}, u32[]{:S(2)}) collective-permute-start(f32[32,1024]{1,0:T(8,128)S(1)} %get-tuple-element.44), channel_id=1, source_target_pairs={{0,0},{1,4},{2,8},{3,12},{4,16},{5,20},{6,24},{7,28},{8,1},{9,5},{... | collective-permute-start | bytes 393224 | tf_op jit(solution)/shard_map/ppermute | solution.py:253
  158.6 31.0 %collective-permute-start.23 = (f32[32,1024]{1,0:T(8,128)S(1)}, f32[32,1024]{1,0:T(8,128)S(1)}, u32[]{:S(2)}, u32[]{:S(2)}) collective-permute-start(f32[32,1024]{1,0:T(8,128)S(1)} %get-tuple-element.41), channel_id=1, source_target_pairs={{0,1},{1,5},{2,9},{3,13},{4,17},{5,21},{6,25},{7,29},{8,2},{9,6},{... | collective-permute-start | bytes 393224 | tf_op jit(solution)/shard_map/ppermute | solution.py:253
  163.4 30.5 %copy-start.8 = (bf16[128,1024]{1,0:T(8,128)(2,1)}, bf16[128,1024]{1,0:T(8,128)(2,1)S(1)}, u32[]{:S(2)}) copy-start(bf16[128,1024]{1,0:T(8,128)(2,1)S(1)} %collective-permute-done.14.rest_2_) | copy-start | bytes 786436
  163.4 27.7 %collective-permute-start.24 = (f32[32,1024]{1,0:T(8,128)S(1)}, f32[32,1024]{1,0:T(8,128)S(1)}, u32[]{:S(2)}, u32[]{:S(2)}) collective-permute-start(f32[32,1024]{1,0:T(8,128)S(1)} %get-tuple-element.43), channel_id=1, source_target_pairs={{0,2},{1,6},{2,10},{3,14},{4,18},{5,22},{6,26},{7,30},{8,3},{9,7},... | collective-permute-start | bytes 393224 | tf_op jit(solution)/shard_map/ppermute | solution.py:253
  163.5 30.4 %copy-start.9 = (bf16[128,1024]{1,0:T(8,128)(2,1)}, bf16[128,1024]{1,0:T(8,128)(2,1)S(1)}, u32[]{:S(2)}) copy-start(bf16[128,1024]{1,0:T(8,128)(2,1)S(1)} %collective-permute-done.16.rest_4_) | copy-start | bytes 786436
  163.5 29.6 %collective-permute-start.25 = (f32[32,1024]{1,0:T(8,128)S(1)}, f32[32,1024]{1,0:T(8,128)S(1)}, u32[]{:S(2)}, u32[]{:S(2)}) collective-permute-start(f32[32,1024]{1,0:T(8,128)S(1)} %get-tuple-element.42), channel_id=1, source_target_pairs={{0,3},{1,7},{2,11},{3,15},{4,19},{5,23},{6,27},{7,31},{8,0},{9,4},... | collective-permute-start | bytes 393224 | tf_op jit(solution)/shard_map/ppermute | solution.py:253
  170.4 23.5 %copy-start.10 = (bf16[128,1024]{1,0:T(8,128)(2,1)}, bf16[128,1024]{1,0:T(8,128)(2,1)S(1)}, u32[]{:S(2)}) copy-start(bf16[128,1024]{1,0:T(8,128)(2,1)S(1)} %collective-permute-done.18.rest_6_) | copy-start | bytes 786436
  170.4 23.4 %collective-permute-start.13 = (bf16[128,1024]{1,0:T(8,128)(2,1)S(1)}, bf16[128,1024]{1,0:T(8,128)(2,1)S(1)}, u32[]{:S(2)}, u32[]{:S(2)}) collective-permute-start(bf16[128,1024]{1,0:T(8,128)(2,1)S(1)} %bitcast.32), channel_id=1, source_target_pairs={{0,1},{1,0},{2,3},{3,2},{4,5},{5,4},{6,7},{7,6},{8,9},{9,8},{10,11... | collective-permute-start | bytes 786440 | tf_op jit(solution)/shard_map/ppermute | solution.py:253
  185.5 8.4 %collective-permute-start.15 = (bf16[128,1024]{1,0:T(8,128)(2,1)S(1)}, bf16[128,1024]{1,0:T(8,128)(2,1)S(1)}, u32[]{:S(2)}, u32[]{:S(2)}) collective-permute-start(bf16[128,1024]{1,0:T(8,128)(2,1)S(1)} %collective-permute-done.14.rest_2_), channel_id=1, source_target_pairs={{0,1},{1,0},{2,3},{3,2},{4,5},{5,4},{6,7},{7,6},{8,9},{9,8},{10,11... | collective-permute-start | bytes 786440 | tf_op jit(solution)/shard_map/ppermute | solution.py:253
  189.5 4.3 %collective-permute-start.17 = (bf16[128,1024]{1,0:T(8,128)(2,1)S(1)}, bf16[128,1024]{1,0:T(8,128)(2,1)S(1)}, u32[]{:S(2)}, u32[]{:S(2)}) collective-permute-start(bf16[128,1024]{1,0:T(8,128)(2,1)S(1)} %collective-permute-done.16.rest_4_), channel_id=1, source_target_pairs={{0,1},{1,0},{2,3},{3,2},{4,5},{5,4},{6,7},{7,6},{8,9},{9,8},{10,11... | collective-permute-start | bytes 786440 | tf_op jit(solution)/shard_map/ppermute | solution.py:253
  191.1 2.8 %collective-permute-start.19 = (bf16[128,1024]{1,0:T(8,128)(2,1)S(1)}, bf16[128,1024]{1,0:T(8,128)(2,1)S(1)}, u32[]{:S(2)}, u32[]{:S(2)}) collective-permute-start(bf16[128,1024]{1,0:T(8,128)(2,1)S(1)} %collective-permute-done.18.rest_6_), channel_id=1, source_target_pairs={{0,1},{1,0},{2,3},{3,2},{4,5},{5,4},{6,7},{7,6},{8,9},{9,8},{10,11... | collective-permute-start | bytes 786440 | tf_op jit(solution)/shard_map/ppermute | solution.py:253
  193.9 0.7 copy-start.11
  193.9 0.8 copy-start.12
  193.9 0.9 copy-start.13
  194.7 0.7 copy-start.14
  198.8 0.9 copy-start.1
